TPU v7x, 32 devices: a whole 2x2x4 slice. The times are simulated.
32 devices in a mesh: grp: 4 (over y, x), gx: 4 (over z), gy: 2 (over core).
Axes of the slice: x: 2, y: 2, z: 4, core: 2. Of those that a mesh axis runs over, the one named last changes fastest.
Arguments:
- coarse_modes: float32 [4, 2, 8, 32, 4096], P('grp', None, None, 'gy', 'gx'), may hold values from -6 to 6
- salinity: float32 [32, 128, 16384], P('grp', 'gy', 'gx'), may hold values from -6 to 6
- viscosity: float32 [4], P('grp'), may hold values from 0.1 to 1
- forcing_gain: float32 [4], P('grp'), may hold values from 0.5 to 2
- diffusivity: float32 [32], P('grp'), may hold values from 0.3 to 1.5
Outputs:
- salinity_next: float32 [32, 128, 16384], P('grp', 'gy', 'gx')
- coarse_next: float32 [4, 2, 8, 32, 4096], P('grp', None, None, 'gy', 'gx')
All inputs are finite; a program needn't handle non-finite values.
Results may differ from a plain program's by a relative error of at most 0.0003.
Values sent between devices are 32-bit elements; how exact they have to be, the bound alone decides.
A program may use at most 192 MiB of HBM per device.

v0:
```python
import math

import jax
import jax.numpy as jnp
from jax import lax
from jax.experimental import pallas as pl
from jax.experimental.pallas import tpu as pltpu
from jax.sharding import PartitionSpec as P

RATIO = 4


fine_step = 0.1


def extended(cells, sides, width):
    for axis, dim in sides:
        count = lax.axis_size(axis)
        head = lax.slice_in_dim(cells, 0, width, axis=dim)
        tail = lax.slice_in_dim(cells, cells.shape[dim] - width, cells.shape[dim], axis=dim)
        cells = jnp.concatenate(
            [
                lax.ppermute(tail, axis, [(i, (i + 1) % count) for i in range(count)]),
                cells,
                lax.ppermute(head, axis, [((i + 1) % count, i) for i in range(count)]),
            ],
            axis=dim,
        )
    return cells


def circle_table(row_count, col_count, period, orient):
    product = (
        lax.broadcasted_iota(jnp.int32, (row_count, col_count), 0)
        * lax.broadcasted_iota(jnp.int32, (row_count, col_count), 1)
        % period
    )
    angle = 2.0 * math.pi / period * product.astype(jnp.float32)
    return (jnp.cos(angle), orient * jnp.sin(angle))


def contract(data, table, form):
    return jnp.einsum(form, data, table, precision=lax.Precision.HIGH)


def fourier_lines(real_part, imag_part, orient, want_imag):
    length = real_part.shape[-1]
    exponent = length.bit_length() - 1
    inner_count = 2 ** ((exponent + 2) // 2)
    outer_count = length // inner_count
    leading = real_part.shape[:-1]
    cos_outer, sin_outer = circle_table(outer_count, outer_count, outer_count, orient)
    cos_twist, sin_twist = circle_table(outer_count, inner_count, length, orient)
    cos_inner, sin_inner = circle_table(inner_count, inner_count, inner_count, orient)
    first_form = "...ba,bk->...ka"
    second_form = "...ka,aj->...jk"
    split_real = real_part.reshape(leading + (outer_count, inner_count))
    section_real = contract(split_real, cos_outer, first_form)
    section_imag = contract(split_real, sin_outer, first_form)
    if imag_part is not None:
        split_imag = imag_part.reshape(leading + (outer_count, inner_count))
        section_real = section_real - contract(split_imag, sin_outer, first_form)
        section_imag = section_imag + contract(split_imag, cos_outer, first_form)
    twist_real = section_real * cos_twist - section_imag * sin_twist
    twist_imag = section_real * sin_twist + section_imag * cos_twist
    norm_factor = length ** (-0.5)
    final_real = (
        contract(twist_real, cos_inner, second_form) - contract(twist_imag, sin_inner, second_form)
    ) * norm_factor
    if not want_imag:
        return final_real.reshape(leading + (length,))
    final_imag = (
        contract(twist_real, sin_inner, second_form) + contract(twist_imag, cos_inner, second_form)
    ) * norm_factor
    return (final_real.reshape(leading + (length,)), final_imag.reshape(leading + (length,)))


def spread_table(cell_count, source_count):
    fine_count = cell_count * RATIO
    source = lax.broadcasted_iota(jnp.int32, (source_count, fine_count), 0)
    fine_cell = lax.broadcasted_iota(jnp.int32, (source_count, fine_count), 1)
    parent = fine_cell // RATIO
    sub_cell = (fine_cell % RATIO).astype(jnp.float32)
    offset = (sub_cell + 0.5) / RATIO - 0.5
    magnitude = jnp.abs(offset)
    own_weight = jnp.where(source == parent + 1, 1.0 - magnitude, 0.0)
    after_weight = jnp.where((source == parent + 2) & (offset > 0), magnitude, 0.0)
    before_weight = jnp.where((source == parent) & (offset < 0), magnitude, 0.0)
    return (own_weight + after_weight + before_weight).astype(jnp.bfloat16)


def average_table(fine_count, weight):
    fine_cell = lax.broadcasted_iota(jnp.int32, (fine_count, fine_count // RATIO), 0)
    coarse_cell = lax.broadcasted_iota(jnp.int32, (fine_count, fine_count // RATIO), 1)
    return jnp.where(fine_cell // RATIO == coarse_cell, weight, 0.0).astype(jnp.bfloat16)


def split_parts(value):
    high = value.astype(jnp.bfloat16)
    return high, (value - high.astype(jnp.float32)).astype(jnp.bfloat16)


def product(left, right):
    return jnp.dot(left, right, preferred_element_type=jnp.float32)


def step_kernel(
    cells_coarse,
    diff_ref,
    centre_ref,
    below_ref,
    above_ref,
    lower_ref,
    upper_ref,
    south_ref,
    north_ref,
    west_ref,
    east_ref,
    rim_ref,
    ty_ref,
    tx_ref,
    ry_ref,
    rx_ref,
    out_ref,
    coarse_ref,
    vel_ref,
    acc_ref,
):
    level = pl.program_id(0)
    last = pl.num_programs(0) - 1
    part = lax.rem(level, RATIO)
    rows, cols = centre_ref.shape[1], centre_ref.shape[2]
    fine = cells_coarse * RATIO
    chunks = cols // fine
    span = tx_ref.shape[0]

    @pl.when(part == 0)
    def _():
        for field in range(rim_ref.shape[0]):
            high, low = split_parts(rim_ref[field, 0])
            along = product(ty_ref[...], high) + product(ty_ref[...], low)
            high, low = split_parts(along)
            for k in range(chunks):
                window = slice(k * cells_coarse, k * cells_coarse + span)
                vel_ref[field, :, k * fine : (k + 1) * fine] = product(
                    high[:, window], tx_ref[...]
                ) + product(low[:, window], tx_ref[...])
        acc_ref[...] = jnp.zeros_like(acc_ref)

    rate = diff_ref[level]
    row_at = lax.broadcasted_iota(jnp.int32, (rows, fine), 0)
    lane_at = lax.broadcasted_iota(jnp.int32, (rows, fine), 1)
    first_lane, last_lane = lane_at == 0, lane_at == fine - 1
    first_row, last_row = row_at == 0, row_at == rows - 1
    bottom, top = level == 0, level == last
    for k in range(chunks):
        start, stop = k * fine, (k + 1) * fine
        centre = centre_ref[0, :, start:stop]
        before = west_ref[0] if k == 0 else centre_ref[0, :, start - 1 : start]
        after = east_ref[0] if k == chunks - 1 else centre_ref[0, :, stop : stop + 1]
        west = jnp.where(first_lane, before, pltpu.roll(centre, 1, 1))
        east = jnp.where(last_lane, after, pltpu.roll(centre, fine - 1, 1))
        south = jnp.where(first_row, south_ref[0, :, start:stop], pltpu.roll(centre, 1, 0))
        north = jnp.where(
            last_row, north_ref[0, :, start:stop], pltpu.roll(centre, rows - 1, 0)
        )
        lower = jnp.where(bottom, lower_ref[0, :, start:stop], below_ref[0, :, start:stop])
        upper = jnp.where(top, upper_ref[0, :, start:stop], above_ref[0, :, start:stop])
        spread = rate * (east + west + north + south + upper + lower - 6.0 * centre)
        advection = (
            vel_ref[0, :, start:stop] * (east - west)
            + vel_ref[1, :, start:stop] * (north - south)
            + vel_ref[2, :, start:stop] * (upper - lower)
        ) * 0.5
        updated = centre + fine_step * (spread - advection)
        out_ref[0, :, start:stop] = updated
        acc_ref[:, start:stop] += vel_ref[3, :, start:stop] - updated

    @pl.when(part == RATIO - 1)
    def _():
        for k in range(chunks):
            high, low = split_parts(acc_ref[:, k * fine : (k + 1) * fine])
            half = product(ry_ref[...], high) + product(ry_ref[...], low)
            high, low = split_parts(half)
            coarse_ref[0, :, k * cells_coarse : (k + 1) * cells_coarse] = product(
                high, rx_ref[...]
            ) + product(low, rx_ref[...])


def fine_update(rimmed, salinity, halos, diffusivity):
    levels, rows, cols = salinity.shape
    fields, quarter, rim_rows, rim_cols = rimmed.shape
    row_count, width = rim_rows - 2, rim_cols - 2
    cells_coarse = min(128, width)
    fine = cells_coarse * RATIO
    span = cells_coarse + 128
    row_pad = -rim_rows % 16
    rimmed = jnp.pad(rimmed, ((0, 0), (0, 0), (0, row_pad), (0, width + 128 - rim_cols)))
    ty = spread_table(row_count, rim_rows + row_pad).T
    tx = spread_table(cells_coarse, span)
    ry = average_table(rows, 1.0 / RATIO).T
    rx = average_table(fine, 1.0 / RATIO / RATIO)

    def fixed(array):
        return pl.BlockSpec(array.shape, lambda i: (0,) * array.ndim)

    def level_block(array):
        return pl.BlockSpec((1,) + array.shape[1:], lambda i: (i, 0, 0))

    slab = (1, rows, cols)
    lower, upper, south, north, west, east = halos
    return pl.pallas_call(
        lambda *refs: step_kernel(cells_coarse, *refs),
        grid=(levels,),
        in_specs=[
            pl.BlockSpec(memory_space=pltpu.SMEM),
            pl.BlockSpec(slab, lambda i: (i, 0, 0)),
            pl.BlockSpec(slab, lambda i: (jnp.maximum(i - 1, 0), 0, 0)),
            pl.BlockSpec(slab, lambda i: (jnp.minimum(i + 1, levels - 1), 0, 0)),
            fixed(lower),
            fixed(upper),
            level_block(south),
            level_block(north),
            level_block(west),
            level_block(east),
            pl.BlockSpec((fields, 1) + rimmed.shape[2:], lambda i: (0, i // RATIO, 0, 0)),
            fixed(ty),
            fixed(tx),
            fixed(ry),
            fixed(rx),
        ],
        out_specs=[
            pl.BlockSpec(slab, lambda i: (i, 0, 0)),
            pl.BlockSpec((1, row_count, width), lambda i: (i // RATIO, 0, 0)),
        ],
        out_shape=[
            jax.ShapeDtypeStruct(salinity.shape, jnp.float32),
            jax.ShapeDtypeStruct((quarter, row_count, width), jnp.float32),
        ],
        scratch_shapes=[
            pltpu.VMEM((fields, rows, cols), jnp.float32),
            pltpu.VMEM((rows, cols), jnp.float32),
        ],
        compiler_params=pltpu.CompilerParams(
            dimension_semantics=("arbitrary",), vmem_limit_bytes=48 * 2**20
        ),
    )(
        diffusivity,
        salinity,
        salinity,
        salinity,
        lower,
        upper,
        south,
        north,
        west,
        east,
        rimmed,
        ty,
        tx,
        ry,
        rx,
    )


def side_layers(cells, axis, dim):
    count = lax.axis_size(axis)
    extent = cells.shape[dim]
    head = lax.slice_in_dim(cells, 0, 1, axis=dim)
    tail = lax.slice_in_dim(cells, extent - 1, extent, axis=dim)
    return (
        lax.ppermute(tail, axis, [(i, (i + 1) % count) for i in range(count)]),
        lax.ppermute(head, axis, [((i + 1) % count, i) for i in range(count)]),
    )


def scatter_columns(lines):
    count = lax.axis_size("gx")
    lead = lines.ndim - 2
    rows, length = lines.shape[-2:]
    pieces = lines.reshape(lines.shape[:-1] + (count, length // count))
    pieces = jnp.moveaxis(pieces, lead + 1, 0)
    landed = lax.all_to_all(pieces, "gx", split_axis=0, concat_axis=0, tiled=True)
    landed = jnp.moveaxis(landed, 0, lead)
    return landed.reshape(lines.shape[:-2] + (count * rows, length // count))


def per_device(coarse_modes, salinity, viscosity, forcing_gain, diffusivity):
    planes = coarse_modes.shape[2]
    row_count = coarse_modes.shape[3]
    width = coarse_modes.shape[4]
    groups = lax.axis_size("grp")
    quarter = planes // groups
    halos = (
        side_layers(salinity, "grp", 0)
        + side_layers(salinity, "gy", 1)
        + side_layers(salinity, "gx", 2)
    )
    pencil = lax.all_to_all(coarse_modes[0], "gx", split_axis=2, concat_axis=3, tiled=True)
    physical = fourier_lines(pencil[0], pencil[1], 1.0, False)
    blocks = scatter_columns(physical)
    received = lax.all_to_all(
        blocks.reshape(groups, quarter, row_count, width),
        "grp",
        split_axis=0,
        concat_axis=0,
        tiled=True,
    )
    rimmed = extended(received, (("gx", 3), ("gy", 2)), 1)
    salinity_next, restricted = fine_update(rimmed, salinity, halos, diffusivity)
    columns = lax.all_to_all(restricted, "gx", split_axis=1, concat_axis=2, tiled=True)
    spec_real, spec_imag = fourier_lines(columns, None, -1.0, True)
    own_spectra = scatter_columns(jnp.stack([spec_real, spec_imag]))
    spectrum = lax.all_to_all(
        jnp.broadcast_to(own_spectra[None], (groups,) + own_spectra.shape),
        "grp",
        split_axis=0,
        concat_axis=0,
        tiled=True,
    )
    spectrum = jnp.moveaxis(spectrum, 0, 1).reshape((2, planes) + own_spectra.shape[2:])
    total_modes = width * lax.axis_size("gx")
    mode_index = lax.axis_index("gx") * width + lax.broadcasted_iota(jnp.int32, (width,), 0)
    wavenumber = jnp.where(mode_index < total_modes // 2, mode_index, mode_index - total_modes)
    scaled_wave = 2.0 * math.pi / total_modes * wavenumber.astype(jnp.float32)
    damping = jnp.exp(-viscosity[0] * scaled_wave * scaled_wave)
    coarse_next = damping * coarse_modes + forcing_gain[0] * spectrum[None]
    return (salinity_next, coarse_next)


def solution(mesh):
    return jax.shard_map(
        per_device,
        mesh=mesh,
        in_specs=(
            P("grp", None, None, "gy", "gx"),
            P("grp", "gy", "gx"),
            P("grp"),
            P("grp"),
            P("grp"),
        ),
        out_specs=(P("grp", "gy", "gx"), P("grp", None, None, "gy", "gx")),
        check_vma=False,
    )
```

profile of v0, /device:TPU:0, one launch (start us, length us, event | category | flops | bytes accessed | tf_op | source)
XLA Modules:
  0.0 171.9 jit_solution(262901731992191959)
XLA Ops:
  0.6 2.8 %copy.59 = f32[1,2,8,16,1024]{4,2,1,3,0:T(8,128)} copy(f32[1,2,8,16,1024]{4,3,2,1,0:T(8,128)} %param.5) | data formatting | bytes 2097152 | tf_op args[0]
  3.4 6.3 %all-to-all-start = ((f32[2,8,16,1024]{3,1,0,2:T(8,128)}), f32[2,8,16,1024]{3,1,0,2:T(8,128)S(1)}, u32[]{:S(2)}, u32[]{:S(2)}) async-start(f32[2,8,16,1024]{3,1,0,2:T(8,128)} %bitcast.96), calls=%async_computation | async-start | bytes 2097152 | tf_op jit(solution)/shard_map/all_to_all | solution.py:299
  9.8 3.1 %fusion.151 = (f32[1,64,4096]{2,1,0:T(8,128)}, f32[1,64,4096]{2,1,0:T(8,128)}) fusion(f32[8,64,4096]{2,1,0:T(8,128)} %refs_3_.1), kind=kLoop, calls=%fused_computation.197 | loop fusion | bytes 4194304 | tf_op jit(solution)/shard_map/slice | solution.py:269
  12.9 1.5 collective-permute-start
  14.3 1.4 collective-permute-start.1
  15.8 1.9 %fusion.149 = (f32[8,64,1]{2,1,0:T(8,128)}, f32[8,64,1]{2,1,0:T(8,128)}) fusion(f32[8,64,4096]{2,1,0:T(8,128)} %refs_3_.1), kind=kLoop, calls=%fused_computation.195 | loop fusion | bytes 8192 | tf_op jit(solution)/shard_map/slice | solution.py:269
  17.7 2.0 %collective-permute-start.4 = (f32[8,64,1]{2,1,0:T(8,128)}, f32[8,64,1]{2,1,0:T(8,128)S(1)}, u32[]{:S(2)}, u32[]{:S(2)}) collective-permute-start(f32[8,64,1]{2,1,0:T(8,128)} %get-tuple-element.7), channel_id=1, source_target_pairs={{0,2},{2,4},{4,6},{6,0},{1,3},{3,5},{5,7},{7,1},{8,10},{10,12},{12... | collective-permute-start | bytes 6152 | tf_op jit(solution)/shard_map/ppermute | solution.py:272
  19.7 0.5 fusion.96
  20.2 0.6 compare_and_fusion
  20.8 0.6 iota_shift-right-logical_fusion
  21.4 0.6 fusion.92
  22.0 0.7 fusion.81
  23.0 18.2 %all-to-all-done = f32[2,8,16,1024]{3,1,0,2:T(8,128)S(1)} async-done(((f32[2,8,16,1024]{3,1,0,2:T(8,128)}), f32[2,8,16,1024]{3,1,0,2:T(8,128)S(1)}, u32[]{:S(2)}, u32[]{:S(2)}) %all-to-all-start) | async-done | bytes 1048608 | tf_op jit(solution)/shard_map/all_to_all | solution.py:299
  41.1 0.7 copy.58
  41.8 0.9 fusion.152
  42.9 1.3 fusion.70
  44.6 1.3 reshape_squeeze.7
  45.9 1.5 convolution_add_fusion
  48.1 0.6 fusion.7
  48.7 0.6 fusion.1
  49.3 1.9 %copy.37 = f32[8,4,128,32]{3,2,1,0:T(8,128)} copy(f32[8,4,128,32]{2,3,1,0:T(8,128)S(1)} %fusion.1) | data formatting | bytes 1048576 | tf_op jit(solution)/shard_map/mul | solution.py:67
  51.3 2.5 %reshape_reshape.6 = f32[8,4,4,1024]{3,2,1,0:T(4,128)S(1)} reshape(f32[8,4,128,32]{3,2,1,0:T(8,128)} %copy.37) | data formatting | bytes 1048576 | tf_op jit(solution)/shard_map/reshape;reshape | solution.py:281
  53.8 1.1 copy.38
  54.9 3.5 %all-to-all-start.1 = ((f32[4,8,4,1024]{3,2,1,0:T(4,128)}), f32[4,8,4,1024]{3,2,1,0:T(4,128)S(1)}, u32[]{:S(2)}, u32[]{:S(2)}) async-start(f32[4,8,4,1024]{3,2,1,0:T(4,128)} %copy.38), calls=%async_computation.1 | async-start | bytes 1048576 | tf_op jit(solution)/shard_map/all_to_all | solution.py:283
  58.4 2.4 %fusion.150 = (f32[8,1,4096]{2,1,0:T(1,128)}, f32[8,1,4096]{2,1,0:T(1,128)}) fusion(f32[8,64,4096]{2,1,0:T(8,128)} %refs_3_.1), kind=kLoop, calls=%fused_computation.196 | loop fusion | bytes 524288 | tf_op jit(solution)/shard_map/slice | solution.py:269
  60.8 11.6 %all-to-all-done.1 = f32[4,8,4,1024]{3,2,1,0:T(4,128)S(1)} async-done(((f32[4,8,4,1024]{3,2,1,0:T(4,128)}), f32[4,8,4,1024]{3,2,1,0:T(4,128)S(1)}, u32[]{:S(2)}, u32[]{:S(2)}) %all-to-all-start.1) | async-done | bytes 524320 | tf_op jit(solution)/shard_map/all_to_all | solution.py:283
  72.4 1.0 reshape_reshape.7
  73.4 3.8 %all-to-all-start.2 = ((f32[4,2,16,1024]{3,2,1,0:T(8,128)}), f32[4,2,16,1024]{3,2,1,0:T(8,128)S(1)}, u32[]{:S(2)}, u32[]{:S(2)}) async-start(f32[4,2,16,1024]{3,2,1,0:T(8,128)} %reshape_reshape.7), calls=%async_computation.2 | async-start | bytes 1048576 | tf_op jit(solution)/shard_map/all_to_all | solution.py:302
  77.3 0.9 add_convert_fusion.refs_12_
  78.2 6.3 %all-to-all-done.2 = f32[4,2,16,1024]{3,2,1,0:T(8,128)S(1)} async-done(((f32[4,2,16,1024]{3,2,1,0:T(8,128)}), f32[4,2,16,1024]{3,2,1,0:T(8,128)S(1)}, u32[]{:S(2)}, u32[]{:S(2)}) %all-to-all-start.2) | async-done | bytes 524320 | tf_op jit(solution)/shard_map/all_to_all | solution.py:302
  84.7 3.8 %collective-permute-start.7 = (f32[4,2,16,1]{3,2,1,0:T(8,128)S(1)}, f32[4,2,16,1]{3,2,1,0:T(8,128)}, u32[]{:S(2)}, u32[]{:S(2)}) collective-permute-start(f32[4,2,16,1]{3,2,1,0:T(8,128)S(1)} %get-tuple-element.16), channel_id=1, source_target_pairs={{2,0},{4,2},{6,4},{0,6},{3,1},{5,3},{7,5},{1,7},{10,8},{12,10},{14... | collective-permute-start | bytes 1544 | tf_op jit(solution)/shard_map/ppermute | solution.py:25
  88.6 2.1 %collective-permute-done.6 = f32[4,2,16,1]{3,2,1,0:T(8,128)S(1)} collective-permute-done((f32[4,2,16,1]{3,2,1,0:T(8,128)S(1)}, f32[4,2,16,1]{3,2,1,0:T(8,128)S(1)}, u32[]{:S(2)}, u32[]{:S(2)}) %collective-permute-start.6) | collective-permute-done | bytes 544 | tf_op jit(solution)/shard_map/ppermute | solution.py:23
  90.7 0.6 copy-done.5
  91.4 1.4 concatenate.7
  92.9 0.5 collective-permute-start.9
  93.4 3.5 %collective-permute-start.5 = (f32[8,64,1]{2,1,0:T(8,128)}, f32[8,64,1]{2,1,0:T(8,128)S(1)}, u32[]{:S(2)}, u32[]{:S(2)}) collective-permute-start(f32[8,64,1]{2,1,0:T(8,128)} %get-tuple-element.6), channel_id=1, source_target_pairs={{2,0},{4,2},{6,4},{0,6},{3,1},{5,3},{7,5},{1,7},{10,8},{12,10},{14... | collective-permute-start | bytes 6152 | tf_op jit(solution)/shard_map/ppermute | solution.py:273
  96.9 0.5 collective-permute-start.3
  97.6 5.4 %collective-permute-done.5.refs_9_ = f32[8,64,1]{2,1,0:T(8,128)S(1)} collective-permute-done((f32[8,64,1]{2,1,0:T(8,128)}, f32[8,64,1]{2,1,0:T(8,128)S(1)}, u32[]{:S(2)}, u32[]{:S(2)}) %collective-permute-start.5) | collective-permute-done | bytes 2080 | tf_op jit(solution)/shard_map/ppermute | solution.py:273
  103.1 26.5 %shard_map.68 = (f32[8,64,4096]{2,1,0:T(8,128)}, f32[2,16,1024]{2,1,0:T(8,128)S(1)}) custom-call(f32[8]{0:T(128)S(1)} %copy-done, f32[8,64,4096]{2,1,0:T(8,128)} %refs_3_.1, f32[8,64,4096]{2,1,0:T(8,128)} %refs_3_.1, f32[8,64,4096]{2,1,0:T(8,128)} %refs_3_.1, f32[1,64,4096]{2,1,0:T(8,128)S(1)} %collective-permute-done.refs_4_, ...), custom_call_target="tpu_custom_call" | custom-call | tf_op jit(solution)/shard_map/pallas_call | solution.py:212
  129.6 0.8 copy.40
  130.3 5.4 %all-to-all-start.3 = ((f32[2,16,1024]{2,0,1:T(2,128)}), f32[2,16,1024]{2,0,1:T(2,128)S(1)}, u32[]{:S(2)}, u32[]{:S(2)}) async-start(f32[2,16,1024]{2,0,1:T(2,128)} %copy.40), calls=%async_computation.3 | async-start | bytes 262144 | tf_op jit(solution)/shard_map/all_to_all | solution.py:311
  135.9 5.8 %all-to-all-done.3 = f32[2,16,1024]{2,0,1:T(2,128)S(1)} async-done(((f32[2,16,1024]{2,0,1:T(2,128)}), f32[2,16,1024]{2,0,1:T(2,128)S(1)}, u32[]{:S(2)}, u32[]{:S(2)}) %all-to-all-start.3) | async-done | bytes 131104 | tf_op jit(solution)/shard_map/all_to_all | solution.py:311
  143.3 0.5 fusion.3
  145.5 9.6 %all_to_all.50 = f32[4,2,2,4,1024]{4,3,2,1,0:T(4,128)S(1)} all-to-all(f32[4,2,2,4,1024]{4,3,2,1,0:T(4,128)S(1)} %copy.44), channel_id=1, replica_groups=mesh['grp'=4,'gx'=4,'gy'=2] {'gx'}, dimensions={0} | all-to-all | bytes 524288 | tf_op jit(solution)/shard_map/all_to_all | solution.py:283
  155.4 1.1 broadcast_in_dim.51
  156.5 3.5 %all-to-all-start.5 = ((f32[4,2,2,16,1024]{4,3,2,1,0:T(8,128)}), f32[4,2,2,16,1024]{4,3,2,1,0:T(8,128)S(1)}, u32[]{:S(2)}, u32[]{:S(2)}) async-start(f32[4,2,2,16,1024]{4,3,2,1,0:T(8,128)} %broadcast_in_dim.51), calls=%async_computation.5 | async-start | bytes 2097152 | tf_op jit(solution)/shard_map/all_to_all | solution.py:314
  161.4 9.3 %all-to-all-done.5 = f32[4,2,2,16,1024]{4,3,2,1,0:T(8,128)S(1)} async-done(((f32[4,2,2,16,1024]{4,3,2,1,0:T(8,128)}), f32[4,2,2,16,1024]{4,3,2,1,0:T(8,128)S(1)}, u32[]{:S(2)}, u32[]{:S(2)}) %all-to-all-start.5) | async-done | bytes 1048608 | tf_op jit(solution)/shard_map/all_to_all | solution.py:314
  170.8 1.1 multiply_add_fusion
  (62 shorter events, 6.0 us)
Async XLA Ops:
  3.4 37.7 %all-to-all-start = ((f32[2,8,16,1024]{3,1,0,2:T(8,128)}), f32[2,8,16,1024]{3,1,0,2:T(8,128)S(1)}, u32[]{:S(2)}, u32[]{:S(2)}) async-start(f32[2,8,16,1024]{3,1,0,2:T(8,128)} %bitcast.96), calls=%async_computation | async-start | bytes 2097152 | tf_op jit(solution)/shard_map/all_to_all | solution.py:299
  12.9 90.2 %collective-permute-start = (f32[1,64,4096]{2,1,0:T(8,128)}, f32[1,64,4096]{2,1,0:T(8,128)S(1)}, u32[]{:S(2)}, u32[]{:S(2)}) collective-permute-start(f32[1,64,4096]{2,1,0:T(8,128)} %get-tuple-element.11), channel_id=1, source_target_pairs={{0,8},{8,16},{16,24},{24,0},{1,9},{9,17},{17,25},{25,1},{2,10},{10... | collective-permute-start | bytes 3145736 | tf_op jit(solution)/shard_map/ppermute | solution.py:272
  14.3 88.7 %collective-permute-start.1 = (f32[1,64,4096]{2,1,0:T(8,128)}, f32[1,64,4096]{2,1,0:T(8,128)S(1)}, u32[]{:S(2)}, u32[]{:S(2)}) collective-permute-start(f32[1,64,4096]{2,1,0:T(8,128)} %get-tuple-element.10), channel_id=1, source_target_pairs={{8,0},{16,8},{24,16},{0,24},{9,1},{17,9},{25,17},{1,25},{10,2},{18... | collective-permute-start | bytes 3145736 | tf_op jit(solution)/shard_map/ppermute | solution.py:273
  17.7 75.7 %collective-permute-start.4 = (f32[8,64,1]{2,1,0:T(8,128)}, f32[8,64,1]{2,1,0:T(8,128)S(1)}, u32[]{:S(2)}, u32[]{:S(2)}) collective-permute-start(f32[8,64,1]{2,1,0:T(8,128)} %get-tuple-element.7), channel_id=1, source_target_pairs={{0,2},{2,4},{4,6},{6,0},{1,3},{3,5},{5,7},{7,1},{8,10},{10,12},{12... | collective-permute-start | bytes 6152 | tf_op jit(solution)/shard_map/ppermute | solution.py:272
  20.2 2.5 %copy-start.8 = (pred[512]{0:T(512)(128)(4,1)}, pred[512]{0:T(512)(128)(4,1)S(1)}, u32[]{:S(2)}) copy-start(pred[512]{0:T(512)(128)(4,1)S(1)} %get-tuple-element.30) | copy-start | bytes 1540
  21.4 1.3 copy-start.6
  22.0 0.7 copy-start.7
  47.3 0.7 copy-start.3
  54.9 17.5 %all-to-all-start.1 = ((f32[4,8,4,1024]{3,2,1,0:T(4,128)}), f32[4,8,4,1024]{3,2,1,0:T(4,128)S(1)}, u32[]{:S(2)}, u32[]{:S(2)}) async-start(f32[4,8,4,1024]{3,2,1,0:T(4,128)} %copy.38), calls=%async_computation.1 | async-start | bytes 1048576 | tf_op jit(solution)/shard_map/all_to_all | solution.py:283
  73.4 15.1 %copy-start.9 = (pred[64]{0:T(512)(128)(4,1)S(1)}, pred[64]{0:T(512)(128)(4,1)}, u32[]{:S(2)}) copy-start(pred[64]{0:T(512)(128)(4,1)} %get-tuple-element.21) | copy-start | bytes 196
  73.4 15.1 %copy-start.10 = (pred[64]{0:T(512)(128)(4,1)S(1)}, pred[64]{0:T(512)(128)(4,1)}, u32[]{:S(2)}) copy-start(pred[64]{0:T(512)(128)(4,1)} %get-tuple-element.20) | copy-start | bytes 196
  73.4 11.1 %all-to-all-start.2 = ((f32[4,2,16,1024]{3,2,1,0:T(8,128)}), f32[4,2,16,1024]{3,2,1,0:T(8,128)S(1)}, u32[]{:S(2)}, u32[]{:S(2)}) async-start(f32[4,2,16,1024]{3,2,1,0:T(8,128)} %reshape_reshape.7), calls=%async_computation.2 | async-start | bytes 1048576 | tf_op jit(solution)/shard_map/all_to_all | solution.py:302
  77.3 19.7 %copy-start.4 = (f32[8,1,4096]{2,1,0:T(1,128)S(1)}, f32[8,1,4096]{2,1,0:T(1,128)}, u32[]{:S(2)}) copy-start(f32[8,1,4096]{2,1,0:T(1,128)} %get-tuple-element.8) | copy-start | bytes 393220
  84.6 3.9 %copy-start.2 = (f32[4,2,16,1024]{3,2,1,0:T(8,128)}, f32[4,2,16,1024]{3,2,1,0:T(8,128)S(1)}, u32[]{:S(2)}) copy-start(f32[4,2,16,1024]{3,2,1,0:T(8,128)S(1)} %all-to-all-done.2) | copy-start | bytes 1572868
  84.6 6.1 %collective-permute-start.6 = (f32[4,2,16,1]{3,2,1,0:T(8,128)S(1)}, f32[4,2,16,1]{3,2,1,0:T(8,128)S(1)}, u32[]{:S(2)}, u32[]{:S(2)}) collective-permute-start(f32[4,2,16,1]{3,2,1,0:T(8,128)S(1)} %get-tuple-element.17), channel_id=1, source_target_pairs={{0,2},{2,4},{4,6},{6,0},{1,3},{3,5},{5,7},{7,1},{8,10},{10,12},{12... | collective-permute-start | bytes 1544 | tf_op jit(solution)/shard_map/ppermute | solution.py:23
  84.7 6.7 %collective-permute-start.7 = (f32[4,2,16,1]{3,2,1,0:T(8,128)S(1)}, f32[4,2,16,1]{3,2,1,0:T(8,128)}, u32[]{:S(2)}, u32[]{:S(2)}) collective-permute-start(f32[4,2,16,1]{3,2,1,0:T(8,128)S(1)} %get-tuple-element.16), channel_id=1, source_target_pairs={{2,0},{4,2},{6,4},{0,6},{3,1},{5,3},{7,5},{1,7},{10,8},{12,10},{14... | collective-permute-start | bytes 1544 | tf_op jit(solution)/shard_map/ppermute | solution.py:25
  90.7 0.6 copy-start.5
  92.7 10.3 %copy-start = (f32[8]{0:T(128)S(1)}, f32[8]{0:T(128)}, u32[]{:S(2)}) copy-start(f32[8]{0:T(128)} %refs_0_.1) | copy-start | bytes 100
  92.8 4.1 %collective-permute-start.8 = (f32[4,2,1,1026]{3,2,1,0:T(1,128)S(1)}, f32[4,2,1,1026]{3,2,1,0:T(1,128)S(1)}, u32[]{:S(2)}, u32[]{:S(2)}) collective-permute-start(f32[4,2,1,1026]{3,2,1,0:T(1,128)S(1)} %get-tuple-element.14), channel_id=1, source_target_pairs={{0,1},{1,0},{2,3},{3,2},{4,5},{5,4},{6,7},{7,6},{8,9},{9,8},{10,11... | collective-permute-start | bytes 98504 | tf_op jit(solution)/shard_map/ppermute | solution.py:23
  92.9 4.0 %collective-permute-start.9 = (f32[4,2,1,1026]{3,2,1,0:T(1,128)S(1)}, f32[4,2,1,1026]{3,2,1,0:T(1,128)S(1)}, u32[]{:S(2)}, u32[]{:S(2)}) collective-permute-start(f32[4,2,1,1026]{3,2,1,0:T(1,128)S(1)} %get-tuple-element.15), channel_id=1, source_target_pairs={{1,0},{0,1},{3,2},{2,3},{5,4},{4,5},{7,6},{6,7},{9,8},{8,9},{11,10... | collective-permute-start | bytes 98504 | tf_op jit(solution)/shard_map/ppermute | solution.py:25
  93.4 9.6 %collective-permute-start.5 = (f32[8,64,1]{2,1,0:T(8,128)}, f32[8,64,1]{2,1,0:T(8,128)S(1)}, u32[]{:S(2)}, u32[]{:S(2)}) collective-permute-start(f32[8,64,1]{2,1,0:T(8,128)} %get-tuple-element.6), channel_id=1, source_target_pairs={{2,0},{4,2},{6,4},{0,6},{3,1},{5,3},{7,5},{1,7},{10,8},{12,10},{14... | collective-permute-start | bytes 6152 | tf_op jit(solution)/shard_map/ppermute | solution.py:273
  96.9 6.1 %collective-permute-start.2 = (f32[8,1,4096]{2,1,0:T(1,128)}, f32[8,1,4096]{2,1,0:T(1,128)S(1)}, u32[]{:S(2)}, u32[]{:S(2)}) collective-permute-start(f32[8,1,4096]{2,1,0:T(1,128)} %get-tuple-element.9), channel_id=1, source_target_pairs={{0,1},{1,0},{2,3},{3,2},{4,5},{5,4},{6,7},{7,6},{8,9},{9,8},{10,11... | collective-permute-start | bytes 393224 | tf_op jit(solution)/shard_map/ppermute | solution.py:272
  96.9 6.1 %collective-permute-start.3 = (f32[8,1,4096]{2,1,0:T(1,128)S(1)}, f32[8,1,4096]{2,1,0:T(1,128)S(1)}, u32[]{:S(2)}, u32[]{:S(2)}) collective-permute-start(f32[8,1,4096]{2,1,0:T(1,128)S(1)} %copy-done.4), channel_id=1, source_target_pairs={{1,0},{0,1},{3,2},{2,3},{5,4},{4,5},{7,6},{6,7},{9,8},{8,9},{11,10... | collective-permute-start | bytes 393224 | tf_op jit(solution)/shard_map/ppermute | solution.py:273
  130.3 11.4 %all-to-all-start.3 = ((f32[2,16,1024]{2,0,1:T(2,128)}), f32[2,16,1024]{2,0,1:T(2,128)S(1)}, u32[]{:S(2)}, u32[]{:S(2)}) async-start(f32[2,16,1024]{2,0,1:T(2,128)} %copy.40), calls=%async_computation.3 | async-start | bytes 262144 | tf_op jit(solution)/shard_map/all_to_all | solution.py:311
  156.5 14.2 %all-to-all-start.5 = ((f32[4,2,2,16,1024]{4,3,2,1,0:T(8,128)}), f32[4,2,2,16,1024]{4,3,2,1,0:T(8,128)S(1)}, u32[]{:S(2)}, u32[]{:S(2)}) async-start(f32[4,2,2,16,1024]{4,3,2,1,0:T(8,128)} %broadcast_in_dim.51), calls=%async_computation.5 | async-start | bytes 2097152 | tf_op jit(solution)/shard_map/all_to_all | solution.py:314
  160.0 10.8 %copy-start.1 = (f32[1,2,8,16,1024]{4,3,2,1,0:T(8,128)S(1)}, f32[1,2,8,16,1024]{4,3,2,1,0:T(8,128)}, u32[]{:S(2)}) copy-start(f32[1,2,8,16,1024]{4,3,2,1,0:T(8,128)} %param.5) | copy-start | bytes 3145732
where the time goes:
time: 173 us; the launch traced here: 172 us
  waiting for transfers between devices  58.7 us (34%)
  starting transfers between devices  36 us (21%)
  Pallas kernels  26.5 us (15%)
  local copies, waits for them, and re-layouts  25.7 us (15%)
  blocking collectives  9.6 us (6%)
  matrix products  7.23 us (4%)
  other arithmetic  5.9 us (3%)
  between operations  2.34 us (1%)
    pallas_call x1, Pallas kernels, fine_update(): pl.pallas_call(lambda *refs: step_kernel(cells_coarse, *refs), grid=(leve...  26.5 us
    all_to_all x1, waiting for transfers between devices, per_device(): lax.all_to_all(coarse_modes[0], 'gx', split_axis=2, concat_axis=3, tiled=...  18.2 us
    all_to_all x1, waiting for transfers between devices, scatter_columns(): lax.all_to_all(pieces, 'gx', split_axis=0, concat_axis=0, tiled=True)  11.6 us
    all_to_all x1, blocking collectives, scatter_columns(): lax.all_to_all(pieces, 'gx', split_axis=0, concat_axis=0, tiled=True)  9.6 us
    all_to_all x1, waiting for transfers between devices, per_device(): lax.all_to_all(jnp.broadcast_to(own_spectra[None], (groups,) + own_spectr...  9.25 us
    slice x3, local copies, waits for them, and re-layouts, side_layers(): head = lax.slice_in_dim(cells, 0, 1, axis=dim)  7.44 us
    dot_general x12, matrix products, contract(): return jnp.einsum(form, data, table, precision=lax.Precision.HIGH)  7.23 us
    all_to_all x1, starting transfers between devices, per_device(): lax.all_to_all(coarse_modes[0], 'gx', split_axis=2, concat_axis=3, tiled=...  6.35 us
  transfers between devices with their start and end apart: 15, of which 7 were waited for; matrix products, arithmetic and copies ran while one was open for 16% of the time, Pallas kernels for 0%

commit v1 on v0

--- a/solution.py
+++ b/solution.py
@@ -2,6 +2,7 @@
 
 import jax
 import jax.numpy as jnp
+import numpy as np
 from jax import lax
 from jax.experimental import pallas as pl
 from jax.experimental.pallas import tpu as pltpu
@@ -13,66 +14,506 @@
 fine_step = 0.1
 
 
-def extended(cells, sides, width):
-    for axis, dim in sides:
-        count = lax.axis_size(axis)
-        head = lax.slice_in_dim(cells, 0, width, axis=dim)
-        tail = lax.slice_in_dim(cells, cells.shape[dim] - width, cells.shape[dim], axis=dim)
-        cells = jnp.concatenate(
-            [
-                lax.ppermute(tail, axis, [(i, (i + 1) % count) for i in range(count)]),
-                cells,
-                lax.ppermute(head, axis, [((i + 1) % count, i) for i in range(count)]),
-            ],
-            axis=dim,
+LANES = 128
+SUBLANES = 8
+MESH = pl.DeviceIdType.MESH
+
+
+def turn_table(rows, cols, period, orient, shift):
+    product = np.outer(np.arange(rows) - shift, np.arange(cols)) % period
+    angle = 2.0 * np.pi / period * product
+    return np.cos(angle), orient * np.sin(angle)
+
+
+def twist_table(length, orient, shift):
+    cosine, sine = turn_table(length // LANES, LANES, length, orient, shift)
+    return (np.stack([cosine, sine]) * length ** (-0.25)).astype(np.float32)
+
+
+def lane_table(length, orient, want_imag):
+    tiles = length // LANES
+    groups = LANES // tiles
+    order = (np.arange(tiles)[None, :] * groups + np.arange(groups)[:, None]).reshape(-1)
+    cosine, sine = turn_table(LANES, LANES, LANES, orient, 0)
+    cosine, sine = cosine[order], sine[order]
+    table = np.concatenate([cosine, -sine], axis=1)
+    if want_imag:
+        table = np.concatenate([table, np.concatenate([sine, cosine], axis=1)], axis=0)
+    table = (table * length ** (-0.25)).astype(np.float32)
+    high = table.astype(jnp.bfloat16)
+    low = (table - high.astype(np.float32)).astype(jnp.bfloat16)
+    return np.concatenate([high, low, high], axis=1)
+
+
+def butterflies(parts, orient):
+    count = len(parts)
+    if count == 1:
+        return parts
+    even = butterflies(parts[0::2], orient)
+    odd = butterflies(parts[1::2], orient)
+    sums, differences = [], []
+    for k in range(count // 2):
+        real, imag = odd[k]
+        if k == 0:
+            turned = (real, imag)
+        elif 4 * k == count:
+            turned = (None if imag is None else -orient * imag, orient * real)
+        else:
+            angle = orient * 2.0 * math.pi * k / count
+            cosine, sine = math.cos(angle), math.sin(angle)
+            if imag is None:
+                turned = (cosine * real, sine * real)
+            else:
+                turned = (cosine * real - sine * imag, sine * real + cosine * imag)
+        first = even[k]
+        sums.append((plus(first[0], turned[0]), plus(first[1], turned[1])))
+        differences.append((minus(first[0], turned[0]), minus(first[1], turned[1])))
+    return sums + differences
+
+
+def plus(left, right):
+    if left is None:
+        return right
+    return left if right is None else left + right
+
+
+def minus(left, right):
+    if right is None:
+        return left
+    return -right if left is None else left - right
+
+
+def split_stack(value):
+    high, low = split_parts(value)
+    return jnp.concatenate([high, high, low], axis=1)
+
+
+def transform_lines(tiles, orient, shift, twist_ref, table_ref, mid_ref):
+    count = len(tiles)
+    bins = butterflies(tiles, orient)
+    for r in range(count):
+        real, imag = bins[(r - shift) % count]
+        cosine, sine = twist_ref[0, r : r + 1, :], twist_ref[1, r : r + 1, :]
+        at = slice(r * SUBLANES, (r + 1) * SUBLANES)
+        if imag is None:
+            mid_ref[0, at, :], mid_ref[1, at, :] = real * cosine, real * sine
+        else:
+            mid_ref[0, at, :] = real * cosine - imag * sine
+            mid_ref[1, at, :] = real * sine + imag * cosine
+    parts = [
+        jnp.concatenate(
+            [mid_ref[k, pl.ds(row, count, stride=SUBLANES), :] for row in range(SUBLANES)], axis=0
         )
-    return cells
-
-
-def circle_table(row_count, col_count, period, orient):
-    product = (
-        lax.broadcasted_iota(jnp.int32, (row_count, col_count), 0)
-        * lax.broadcasted_iota(jnp.int32, (row_count, col_count), 1)
-        % period
+        for k in range(2)
+    ]
+    stacked = split_stack(jnp.concatenate(parts, axis=1))
+    return lax.dot_general(
+        table_ref[...], stacked, (((1,), (1,)), ((), ())), preferred_element_type=jnp.float32
     )
-    angle = 2.0 * math.pi / period * product.astype(jnp.float32)
-    return (jnp.cos(angle), orient * jnp.sin(angle))
-
-
-def contract(data, table, form):
-    return jnp.einsum(form, data, table, precision=lax.Precision.HIGH)
-
-
-def fourier_lines(real_part, imag_part, orient, want_imag):
-    length = real_part.shape[-1]
-    exponent = length.bit_length() - 1
-    inner_count = 2 ** ((exponent + 2) // 2)
-    outer_count = length // inner_count
-    leading = real_part.shape[:-1]
-    cos_outer, sin_outer = circle_table(outer_count, outer_count, outer_count, orient)
-    cos_twist, sin_twist = circle_table(outer_count, inner_count, length, orient)
-    cos_inner, sin_inner = circle_table(inner_count, inner_count, inner_count, orient)
-    first_form = "...ba,bk->...ka"
-    second_form = "...ka,aj->...jk"
-    split_real = real_part.reshape(leading + (outer_count, inner_count))
-    section_real = contract(split_real, cos_outer, first_form)
-    section_imag = contract(split_real, sin_outer, first_form)
-    if imag_part is not None:
-        split_imag = imag_part.reshape(leading + (outer_count, inner_count))
-        section_real = section_real - contract(split_imag, sin_outer, first_form)
-        section_imag = section_imag + contract(split_imag, cos_outer, first_form)
-    twist_real = section_real * cos_twist - section_imag * sin_twist
-    twist_imag = section_real * sin_twist + section_imag * cos_twist
-    norm_factor = length ** (-0.5)
-    final_real = (
-        contract(twist_real, cos_inner, second_form) - contract(twist_imag, sin_inner, second_form)
-    ) * norm_factor
-    if not want_imag:
-        return final_real.reshape(leading + (length,))
-    final_imag = (
-        contract(twist_real, sin_inner, second_form) + contract(twist_imag, cos_inner, second_form)
-    ) * norm_factor
-    return (final_real.reshape(leading + (length,)), final_imag.reshape(leading + (length,)))
+
+
+def natural_tiles(result, count, turn_ref):
+    groups = LANES // count
+    group_at = lax.broadcasted_iota(jnp.int32, (count, LANES), 1) // count
+    for tile in range(SUBLANES // groups):
+        lanes = slice(tile * LANES, (tile + 1) * LANES)
+        pieces = [result[k * count : (k + 1) * count, lanes] for k in range(groups)]
+        for row in range(groups):
+            line = None
+            for k in range(groups):
+                shift = count * (k - row) % LANES
+                moved = pieces[k] if shift == 0 else pltpu.roll(pieces[k], shift, 1)
+                line = moved if line is None else jnp.where(group_at == k, moved, line)
+            start = (tile * groups + row) * count
+            turn_ref[start : start + count, :] = line
+    return [turn_ref[pl.ds(u, SUBLANES, stride=count), :] for u in range(count)]
+
+
+def greet(groups, columns, neighbours):
+    barrier = pltpu.get_barrier_semaphore()
+    mine, at = lax.axis_index("grp"), lax.axis_index("gx")
+    total = 0
+    for d in range(groups):
+        for e in range(columns):
+            if d == 0 and e == 0:
+                continue
+            pl.semaphore_signal(
+                barrier,
+                inc=1,
+                device_id={"grp": lax.rem(mine + d, groups), "gx": lax.rem(at + e, columns)},
+                device_id_type=MESH,
+            )
+            total += 1
+    for neighbour in neighbours:
+        pl.semaphore_signal(barrier, inc=1, device_id={"gy": neighbour}, device_id_type=MESH)
+        total += 1
+    pl.semaphore_wait(barrier, total)
+
+
+def forward_kernel(
+    groups,
+    columns,
+    halves_y,
+    modes_ref,
+    twist_ref,
+    table_ref,
+    rim_ref,
+    pencil,
+    mid,
+    turn,
+    lines,
+    landed,
+    side_out,
+    side_in,
+    send_one,
+    recv_one,
+    own_sem,
+    send_two,
+    recv_two,
+    side_send,
+    side_recv,
+):
+    mine, at, half = lax.axis_index("grp"), lax.axis_index("gx"), lax.axis_index("gy")
+    above, below = lax.rem(half + 1, halves_y), lax.rem(half + halves_y - 1, halves_y)
+    planes, rows, width = modes_ref.shape[1:]
+    quarter = planes // groups
+    row_blocks = rows // SUBLANES
+    blocks = quarter * row_blocks
+    turns = pencil.shape[0]
+    count = pencil.shape[3] // LANES
+    span = width + LANES
+    greet(groups, columns, (above, below))
+
+    def place(block):
+        group, inner = block // blocks, lax.rem(block, blocks)
+        plane = inner // row_blocks
+        row = pl.multiple_of(lax.rem(inner, row_blocks) * SUBLANES, SUBLANES)
+        return group, inner, plane, row
+
+    def first_copy(i, d):
+        other = lax.rem(at + d, columns)
+        group, _, plane, row = place(other + columns * i)
+        source = modes_ref.at[:, group * quarter + plane, pl.ds(row, SUBLANES), :]
+        target = pencil.at[i, :, :, pl.ds(pl.multiple_of(at * width, LANES), width)]
+        if d == 0:
+            return pltpu.make_async_copy(source, target, own_sem.at[i])
+        return pltpu.make_async_remote_copy(
+            src_ref=source,
+            dst_ref=target,
+            send_sem=send_one.at[i, d],
+            recv_sem=recv_one.at[i, d],
+            device_id={"gx": other},
+            device_id_type=MESH,
+        )
+
+    for i in range(turns):
+        for d in range(columns):
+            first_copy(i, (d + 1) % columns).start()
+
+    def second_copy(i, b):
+        group, inner, plane, row = place(at + columns * i)
+        source = lines.at[i, :, pl.ds(b * width, span)]
+        target = landed.at[mine, plane, pl.ds(row, SUBLANES), :]
+        remote = lambda: pltpu.make_async_remote_copy(
+            src_ref=source,
+            dst_ref=target,
+            send_sem=send_two.at[i, b],
+            recv_sem=recv_two.at[mine, inner],
+            device_id={"grp": group, "gx": b},
+            device_id_type=MESH,
+        )
+        local = lambda: pltpu.make_async_copy(source, target, recv_two.at[mine, inner])
+        stays = jnp.logical_and(group == mine, at == b)
+        return remote, local, stays
+
+    def one_turn(i, carry):
+        for d in range(columns):
+            if d == 0:
+                first_copy(i, 0).wait()
+            else:
+                first_copy(i, d).wait_recv()
+        tiles = [
+            tuple(pencil[i, k, :, p * LANES : (p + 1) * LANES] for k in range(2))
+            for p in range(count)
+        ]
+        result = transform_lines(tiles, 1.0, 1, twist_ref, table_ref, mid)
+        for u, tile in enumerate(natural_tiles(result, count, turn)):
+            lines[i, :, u * LANES : (u + 1) * LANES] = tile
+            if u == 0:
+                lines[i, :, count * LANES : (count + 1) * LANES] = tile
+        for b in range(columns):
+            remote, local, stays = second_copy(i, b)
+            pl.when(stays)(lambda: local().start())
+            pl.when(jnp.logical_not(stays))(lambda: remote().start())
+        return carry
+
+    lax.fori_loop(0, turns, one_turn, 0)
+    for field in range(groups):
+        for inner in range(blocks):
+            plane, row = inner // row_blocks, inner % row_blocks * SUBLANES
+            target = landed.at[field, plane, pl.ds(row, SUBLANES), :]
+            pltpu.make_async_copy(target, target, recv_two.at[field, inner]).wait()
+    for field in range(groups):
+        for plane in range(quarter):
+            k = field * quarter + plane
+            side_out[0, k : k + 1, :] = landed[field, plane, rows - 1 : rows, :]
+            side_out[1, k : k + 1, :] = landed[field, plane, 0:1, :]
+    sides = [
+        pltpu.make_async_remote_copy(
+            src_ref=side_out.at[k],
+            dst_ref=side_in.at[k],
+            send_sem=side_send.at[k],
+            recv_sem=side_recv.at[k],
+            device_id={"gy": (above, below)[k]},
+            device_id_type=MESH,
+        )
+        for k in range(2)
+    ]
+    for side in sides:
+        side.start()
+    for field in range(groups):
+        for plane in range(quarter):
+            rim_ref[field, plane, 0:rows, :] = landed[field, plane]
+    for side in sides:
+        side.wait()
+    rest = rim_ref.shape[2] - rows - 2
+    for field in range(groups):
+        for plane in range(quarter):
+            k = field * quarter + plane
+            tail = jnp.concatenate(
+                [side_in[0, k : k + 1, :], side_in[1, k : k + 1, :], jnp.zeros((rest, span), jnp.float32)],
+                axis=0,
+            )
+            rim_ref[field, plane, rows:, :] = tail
+    for i in range(turns):
+        for d in range(1, columns):
+            first_copy(i, d).wait_send()
+        for b in range(columns):
+            remote, _, stays = second_copy(i, b)
+            pl.when(jnp.logical_not(stays))(lambda: remote().wait_send())
+
+
+def forward(modes, groups, columns, halves_y):
+    _, planes, rows, width = modes.shape
+    length = width * columns
+    quarter = planes // groups
+    blocks = quarter * (rows // SUBLANES)
+    turns = groups * blocks // columns
+    count = length // LANES
+    span = width + LANES
+    deep = -(-(rows + 2) // 16) * 16
+    twist = twist_table(length, 1.0, 1)
+    table = lane_table(length, 1.0, False)
+    vmem = pl.BlockSpec(memory_space=pltpu.VMEM)
+    dma = pltpu.SemaphoreType.DMA
+    return pl.pallas_call(
+        lambda *refs: forward_kernel(groups, columns, halves_y, *refs),
+        name="forward_lines",
+        out_shape=jax.ShapeDtypeStruct((groups, quarter, deep, span), jnp.float32),
+        in_specs=[vmem] * 3,
+        out_specs=vmem,
+        scratch_shapes=[
+            pltpu.VMEM((turns, 2, SUBLANES, length), jnp.float32),
+            pltpu.VMEM((2, SUBLANES * count, LANES), jnp.float32),
+            pltpu.VMEM((SUBLANES * count, LANES), jnp.float32),
+            pltpu.VMEM((turns, SUBLANES, length + LANES), jnp.float32),
+            pltpu.VMEM((groups, quarter, rows, span), jnp.float32),
+            pltpu.VMEM((2, groups * quarter, span), jnp.float32),
+            pltpu.VMEM((2, groups * quarter, span), jnp.float32),
+            dma((turns, columns)),
+            dma((turns, columns)),
+            dma((turns,)),
+            dma((turns, columns)),
+            dma((groups, blocks)),
+            dma((2,)),
+            dma((2,)),
+        ],
+        compiler_params=pltpu.CompilerParams(
+            collective_id=0, has_side_effects=True, vmem_limit_bytes=32 * 2**20
+        ),
+        cost_estimate=pl.CostEstimate(flops=10**9, bytes_accessed=10**8, transcendentals=0),
+    )(modes, twist, table)
+
+
+def backward_kernel(
+    groups,
+    columns,
+    rates_ref,
+    cells_ref,
+    modes_ref,
+    damp_ref,
+    twist_ref,
+    table_ref,
+    out_ref,
+    pencil,
+    mid,
+    turn,
+    lines,
+    spectrum,
+    send_one,
+    recv_one,
+    send_two,
+    recv_two,
+    send_three,
+):
+    mine, at = lax.axis_index("grp"), lax.axis_index("gx")
+    planes, rows, width = modes_ref.shape[1:]
+    quarter = planes // groups
+    row_blocks = rows // SUBLANES
+    blocks = quarter * row_blocks
+    slots = pencil.shape[0]
+    count = pencil.shape[2] // LANES
+    greet(groups, columns, ())
+
+    def where_is(block):
+        return block // row_blocks, block % row_blocks * SUBLANES
+
+    def to_worker(block):
+        worker, slot = block % columns, block // columns
+        plane, row = where_is(block)
+        source = cells_ref.at[plane, pl.ds(row, SUBLANES), :]
+        target = pencil.at[slot, :, pl.ds(pl.multiple_of(at * width, LANES), width)]
+        remote = lambda: pltpu.make_async_remote_copy(
+            src_ref=source,
+            dst_ref=target,
+            send_sem=send_one.at[block],
+            recv_sem=recv_one.at[slot, at],
+            device_id={"gx": worker},
+            device_id_type=MESH,
+        )
+        local = lambda: pltpu.make_async_copy(source, target, recv_one.at[slot, at])
+        return remote, local, at == worker
+
+    for block in range(blocks):
+        remote, local, stays = to_worker(block)
+        pl.when(stays)(lambda: local().start())
+        pl.when(jnp.logical_not(stays))(lambda: remote().start())
+
+    def to_owner(slot, b):
+        block = at + columns * slot
+        plane, row = block // row_blocks, lax.rem(block, row_blocks) * SUBLANES
+        row = pl.multiple_of(row, SUBLANES)
+        source = lines.at[slot, :, :, pl.ds(b * width, width)]
+        target = spectrum.at[:, mine * quarter + plane, pl.ds(row, SUBLANES), :]
+        remote = lambda: pltpu.make_async_remote_copy(
+            src_ref=source,
+            dst_ref=target,
+            send_sem=send_two.at[slot, b],
+            recv_sem=recv_two.at[mine, block],
+            device_id={"gx": b},
+            device_id_type=MESH,
+        )
+        local = lambda: pltpu.make_async_copy(source, target, recv_two.at[mine, block])
+        return remote, local, at == b
+
+    for slot in range(slots):
+
+        def work(slot=slot):
+            for e in range(columns):
+                target = pencil.at[slot, :, pl.ds(e * width, width)]
+                pltpu.make_async_copy(target, target, recv_one.at[slot, e]).wait()
+            tiles = [(pencil[slot, :, u * LANES : (u + 1) * LANES], None) for u in range(count)]
+            result = transform_lines(tiles, -1.0, 0, twist_ref, table_ref, mid)
+            for k in range(2):
+                part = result[k * LANES : (k + 1) * LANES]
+                for u, tile in enumerate(natural_tiles(part, count, turn)):
+                    lines[slot, k, :, u * LANES : (u + 1) * LANES] = tile
+            for b in range(columns):
+                remote, local, stays = to_owner(slot, b)
+                pl.when(stays)(lambda: local().start())
+                pl.when(jnp.logical_not(stays))(lambda: remote().start())
+
+        if blocks % columns == 0:
+            work()
+        else:
+            pl.when(at + columns * slot < blocks)(work)
+
+    def arrival(group, block):
+        plane, row = where_is(block)
+        target = spectrum.at[:, group * quarter + plane, pl.ds(row, SUBLANES), :]
+        return pltpu.make_async_copy(target, target, recv_two.at[group, block])
+
+    def onward(block, d):
+        plane, row = where_is(block)
+        target = spectrum.at[:, mine * quarter + plane, pl.ds(row, SUBLANES), :]
+        return pltpu.make_async_remote_copy(
+            src_ref=target,
+            dst_ref=target,
+            send_sem=send_three.at[block, d],
+            recv_sem=recv_two.at[mine, block],
+            device_id={"grp": lax.rem(mine + d, groups)},
+            device_id_type=MESH,
+        )
+
+    def finish(group, block):
+        plane, row = where_is(block)
+        index = group * quarter + plane
+        for k in range(2):
+            at_rows = pl.ds(row, SUBLANES)
+            out_ref[k, index, at_rows, :] = (
+                damp_ref[...] * modes_ref[k, index, at_rows, :]
+                + rates_ref[0] * spectrum[k, index, at_rows, :]
+            )
+
+    for block in range(blocks):
+        arrival(mine, block).wait()
+        for d in range(1, groups):
+            onward(block, d).start()
+    for block in range(blocks):
+        finish(mine, block)
+    for block in range(blocks):
+        for d in range(1, groups):
+            group = lax.rem(mine + d, groups)
+            arrival(group, block).wait()
+            finish(group, block)
+    for block in range(blocks):
+        remote, _, stays = to_worker(block)
+        pl.when(jnp.logical_not(stays))(lambda: remote().wait_send())
+        for d in range(1, groups):
+            onward(block, d).wait_send()
+    for slot in range(slots):
+        for b in range(columns):
+            remote, _, stays = to_owner(slot, b)
+            sent = jnp.logical_not(stays)
+            if blocks % columns:
+                sent = jnp.logical_and(sent, at + columns * slot < blocks)
+            pl.when(sent)(lambda: remote().wait_send())
+
+
+def backward(gain, cells, modes, damping, groups, columns):
+    _, planes, rows, width = modes.shape
+    length = width * columns
+    quarter = planes // groups
+    blocks = quarter * (rows // SUBLANES)
+    slots = -(-blocks // columns)
+    count = length // LANES
+    twist = twist_table(length, -1.0, 0)
+    table = lane_table(length, -1.0, True)
+    vmem = pl.BlockSpec(memory_space=pltpu.VMEM)
+    dma = pltpu.SemaphoreType.DMA
+    return pl.pallas_call(
+        lambda *refs: backward_kernel(groups, columns, *refs),
+        name="backward_lines",
+        out_shape=jax.ShapeDtypeStruct(modes.shape, jnp.float32),
+        in_specs=[pl.BlockSpec(memory_space=pltpu.SMEM)] + [vmem] * 5,
+        out_specs=vmem,
+        scratch_shapes=[
+            pltpu.VMEM((slots, SUBLANES, length), jnp.float32),
+            pltpu.VMEM((2, SUBLANES * count, LANES), jnp.float32),
+            pltpu.VMEM((SUBLANES * count, LANES), jnp.float32),
+            pltpu.VMEM((slots, 2, SUBLANES, length), jnp.float32),
+            pltpu.VMEM(modes.shape, jnp.float32),
+            dma((blocks,)),
+            dma((slots, columns)),
+            dma((slots, columns)),
+            dma((groups, blocks)),
+            dma((blocks, groups)),
+        ],
+        compiler_params=pltpu.CompilerParams(
+            collective_id=1, has_side_effects=True, vmem_limit_bytes=32 * 2**20
+        ),
+        cost_estimate=pl.CostEstimate(flops=10**9, bytes_accessed=5 * 10**7, transcendentals=0),
+    )(gain, cells, modes, damping, twist, table)
 
 
 def spread_table(cell_count, source_count):
@@ -86,6 +527,20 @@
     own_weight = jnp.where(source == parent + 1, 1.0 - magnitude, 0.0)
     after_weight = jnp.where((source == parent + 2) & (offset > 0), magnitude, 0.0)
     before_weight = jnp.where((source == parent) & (offset < 0), magnitude, 0.0)
+    return (own_weight + after_weight + before_weight).astype(jnp.bfloat16)
+
+
+def rows_table(row_count, source_count):
+    source = lax.broadcasted_iota(jnp.int32, (row_count * RATIO, source_count), 1)
+    fine_row = lax.broadcasted_iota(jnp.int32, (row_count * RATIO, source_count), 0)
+    parent = fine_row // RATIO
+    offset = ((fine_row % RATIO).astype(jnp.float32) + 0.5) / RATIO - 0.5
+    magnitude = jnp.abs(offset)
+    before = jnp.where(parent == 0, row_count, parent - 1)
+    after = jnp.where(parent == row_count - 1, row_count + 1, parent + 1)
+    own_weight = jnp.where(source == parent, 1.0 - magnitude, 0.0)
+    after_weight = jnp.where((source == after) & (offset > 0), magnitude, 0.0)
+    before_weight = jnp.where((source == before) & (offset < 0), magnitude, 0.0)
     return (own_weight + after_weight + before_weight).astype(jnp.bfloat16)
 
 
@@ -190,13 +645,11 @@
 def fine_update(rimmed, salinity, halos, diffusivity):
     levels, rows, cols = salinity.shape
     fields, quarter, rim_rows, rim_cols = rimmed.shape
-    row_count, width = rim_rows - 2, rim_cols - 2
+    row_count, width = rows // RATIO, cols // RATIO
     cells_coarse = min(128, width)
     fine = cells_coarse * RATIO
     span = cells_coarse + 128
-    row_pad = -rim_rows % 16
-    rimmed = jnp.pad(rimmed, ((0, 0), (0, 0), (0, row_pad), (0, width + 128 - rim_cols)))
-    ty = spread_table(row_count, rim_rows + row_pad).T
+    ty = rows_table(row_count, rim_rows)
     tx = spread_table(cells_coarse, span)
     ry = average_table(rows, 1.0 / RATIO).T
     rx = average_table(fine, 1.0 / RATIO / RATIO)
@@ -274,58 +727,23 @@
     )
 
 
-def scatter_columns(lines):
-    count = lax.axis_size("gx")
-    lead = lines.ndim - 2
-    rows, length = lines.shape[-2:]
-    pieces = lines.reshape(lines.shape[:-1] + (count, length // count))
-    pieces = jnp.moveaxis(pieces, lead + 1, 0)
-    landed = lax.all_to_all(pieces, "gx", split_axis=0, concat_axis=0, tiled=True)
-    landed = jnp.moveaxis(landed, 0, lead)
-    return landed.reshape(lines.shape[:-2] + (count * rows, length // count))
-
-
 def per_device(coarse_modes, salinity, viscosity, forcing_gain, diffusivity):
-    planes = coarse_modes.shape[2]
-    row_count = coarse_modes.shape[3]
     width = coarse_modes.shape[4]
-    groups = lax.axis_size("grp")
-    quarter = planes // groups
+    groups, columns = lax.axis_size("grp"), lax.axis_size("gx")
     halos = (
         side_layers(salinity, "grp", 0)
         + side_layers(salinity, "gy", 1)
         + side_layers(salinity, "gx", 2)
     )
-    pencil = lax.all_to_all(coarse_modes[0], "gx", split_axis=2, concat_axis=3, tiled=True)
-    physical = fourier_lines(pencil[0], pencil[1], 1.0, False)
-    blocks = scatter_columns(physical)
-    received = lax.all_to_all(
-        blocks.reshape(groups, quarter, row_count, width),
-        "grp",
-        split_axis=0,
-        concat_axis=0,
-        tiled=True,
-    )
-    rimmed = extended(received, (("gx", 3), ("gy", 2)), 1)
+    rimmed = forward(coarse_modes[0], groups, columns, lax.axis_size("gy"))
     salinity_next, restricted = fine_update(rimmed, salinity, halos, diffusivity)
-    columns = lax.all_to_all(restricted, "gx", split_axis=1, concat_axis=2, tiled=True)
-    spec_real, spec_imag = fourier_lines(columns, None, -1.0, True)
-    own_spectra = scatter_columns(jnp.stack([spec_real, spec_imag]))
-    spectrum = lax.all_to_all(
-        jnp.broadcast_to(own_spectra[None], (groups,) + own_spectra.shape),
-        "grp",
-        split_axis=0,
-        concat_axis=0,
-        tiled=True,
-    )
-    spectrum = jnp.moveaxis(spectrum, 0, 1).reshape((2, planes) + own_spectra.shape[2:])
-    total_modes = width * lax.axis_size("gx")
-    mode_index = lax.axis_index("gx") * width + lax.broadcasted_iota(jnp.int32, (width,), 0)
+    total_modes = width * columns
+    mode_index = lax.axis_index("gx") * width + lax.broadcasted_iota(jnp.int32, (1, width), 1)
     wavenumber = jnp.where(mode_index < total_modes // 2, mode_index, mode_index - total_modes)
     scaled_wave = 2.0 * math.pi / total_modes * wavenumber.astype(jnp.float32)
     damping = jnp.exp(-viscosity[0] * scaled_wave * scaled_wave)
-    coarse_next = damping * coarse_modes + forcing_gain[0] * spectrum[None]
-    return (salinity_next, coarse_next)
+    coarse_next = backward(forcing_gain, restricted, coarse_modes[0], damping, groups, columns)
+    return (salinity_next, coarse_next[None])
 
 
 def solution(mesh):

time: 173 us -> 118 us (0.68)
  Pallas kernels: 26.5 us -> 91 us
  waiting for transfers between devices: 58.7 us -> 4.06 us
  starting transfers between devices: 36 us -> 8.34 us
  local copies, waits for them, and re-layouts: 25.7 us -> 9.86 us
  blocking collectives: 9.6 us -> 0 us
  matrix products: 7.23 us -> 0 us
  other arithmetic: 5.9 us -> 0.68 us
    pallas_call x0 -> x2, Pallas kernels: none -> 64.5 us  [the longest x1 37.6 us: forward(): pl.pallas_call(lambda *refs: forward_kernel(groups, columns, halves_y, *r...]
    all_to_all x5 -> x0, waiting for transfers between devices: 51.2 us -> none  [the longest x1 18.2 us: per_device(): lax.all_to_all(coarse_modes[0], 'gx', split_axis=2, concat_axis=3, tiled=...]
    all_to_all x5 -> x0, starting transfers between devices: 22.6 us -> none  [the longest x1 6.35 us: per_device(): lax.all_to_all(coarse_modes[0], 'gx', split_axis=2, concat_axis=3, tiled=...]
    all_to_all x1 -> x0, blocking collectives: 9.6 us -> none  [scatter_columns(): lax.all_to_all(pieces, 'gx', split_axis=0, concat_axis=0, tiled=True)]
    dot_general x12 -> x0, matrix products: 7.23 us -> none  [contract(): return jnp.einsum(form, data, table, precision=lax.Precision.HIGH)]
    another operation x6 -> x0, local copies, waits for them, and re-layouts: 5.46 us -> none  [the longest x1 2.49 us: scatter_columns(): pieces = lines.reshape(lines.shape[:-1] + (count, length // count))]
    ppermute x3, waiting for transfers between devices: 5.41 us -> 0.01 us  [side_layers(): lax.ppermute(head, axis, [((i + 1) % count, i) for i in range(count)])]
    ppermute x4 -> x0, starting transfers between devices: 4.41 us -> none  [the longest x2 4.31 us: extended(): lax.ppermute(head, axis, [((i + 1) % count, i) for i in range(count)])]
  transfers between devices with their start and end apart: 15 -> 6, of which waited for: 7 -> 1; matrix products, arithmetic and copies ran while one was open for 16% -> 3% of each run, Pallas kernels for 0% -> 32%
where the time goes in v1:
time: 118 us; the launch traced here: 116 us
  Pallas kernels  91 us (77%)
  local copies, waits for them, and re-layouts  9.86 us (8%)
  starting transfers between devices  8.34 us (7%)
  waiting for transfers between devices  4.06 us (3%)
  between operations  2.13 us (2%)
    pallas_call x1, Pallas kernels, forward(): pl.pallas_call(lambda *refs: forward_kernel(groups, columns, halves_y, *r...  37.6 us
    pallas_call x1, Pallas kernels, backward(): pl.pallas_call(lambda *refs: backward_kernel(groups, columns, *refs), nam...  26.9 us
    pallas_call x1, Pallas kernels, fine_update(): pl.pallas_call(lambda *refs: step_kernel(cells_coarse, *refs), grid=(leve...  26.5 us
    slice x3, local copies, waits for them, and re-layouts, side_layers(): head = lax.slice_in_dim(cells, 0, 1, axis=dim)  5.96 us
    ppermute x3, starting transfers between devices, side_layers(): lax.ppermute(tail, axis, [(i, (i + 1) % count) for i in range(count)])  5.14 us
    ppermute x3, waiting for transfers between devices, side_layers(): lax.ppermute(tail, axis, [(i, (i + 1) % count) for i in range(count)])  4.06 us
    unnamed x15, local copies, waits for them, and re-layouts  3.9 us
    ppermute x3, starting transfers between devices, side_layers(): lax.ppermute(head, axis, [((i + 1) % count, i) for i in range(count)])  3.2 us
  transfers between devices with their start and end apart: 6, of which 1 were waited for; matrix products, arithmetic and copies ran while one was open for 3% of the time, Pallas kernels for 32%

profile of v1, /device:TPU:0, one launch (start us, length us, event | category | flops | bytes accessed | tf_op | source)
XLA Modules:
  0.0 116.1 jit_solution(3121577286537284349)
XLA Ops:
  0.6 0.0 copy-start
  0.6 3.1 %fusion.19 = (f32[1,64,4096]{2,1,0:T(8,128)}, f32[1,64,4096]{2,1,0:T(8,128)}) fusion(f32[8,64,4096]{2,1,0:T(8,128)} %refs_3_.1), kind=kLoop, calls=%fused_computation.52 | loop fusion | bytes 4194304 | tf_op jit(solution)/shard_map/slice | solution.py:722
  3.7 3.0 %collective-permute-start = (f32[1,64,4096]{2,1,0:T(8,128)}, f32[1,64,4096]{2,1,0:T(8,128)S(1)}, u32[]{:S(2)}, u32[]{:S(2)}) collective-permute-start(f32[1,64,4096]{2,1,0:T(8,128)} %get-tuple-element.11), channel_id=1, source_target_pairs={{0,8},{8,16},{16,24},{24,0},{1,9},{9,17},{17,25},{25,1},{2,10},{10... | collective-permute-start | bytes 3145736 | tf_op jit(solution)/shard_map/ppermute | solution.py:725
  6.7 1.0 collective-permute-start.1
  7.6 1.2 fusion.17
  8.8 2.1 %collective-permute-start.4 = (f32[8,64,1]{2,1,0:T(8,128)S(1)}, f32[8,64,1]{2,1,0:T(8,128)S(1)}, u32[]{:S(2)}, u32[]{:S(2)}) collective-permute-start(f32[8,64,1]{2,1,0:T(8,128)S(1)} %get-tuple-element.7), channel_id=1, source_target_pairs={{0,2},{2,4},{4,6},{6,0},{1,3},{3,5},{5,7},{7,1},{8,10},{10,12},{12... | collective-permute-start | bytes 6152 | tf_op jit(solution)/shard_map/ppermute | solution.py:725
  10.9 1.7 %fusion.18 = (f32[8,1,4096]{2,1,0:T(1,128)S(1)}, f32[8,1,4096]{2,1,0:T(1,128)S(1)}) fusion(f32[8,64,4096]{2,1,0:T(8,128)} %refs_3_.1), kind=kLoop, calls=%fused_computation.51 | loop fusion | bytes 524288 | tf_op jit(solution)/shard_map/slice | solution.py:722
  12.6 0.1 collective-permute-start.2
  12.7 0.5 collective-permute-start.3
  13.9 0.1 add_convert_fusion.1.refs_11_
  14.1 0.3 select_convert_fusion.refs_14_
  14.4 0.2 add_convert_fusion.refs_12_
  14.6 4.1 %collective-permute-done.4.refs_8_ = f32[8,64,1]{2,1,0:T(8,128)S(1)} collective-permute-done((f32[8,64,1]{2,1,0:T(8,128)S(1)}, f32[8,64,1]{2,1,0:T(8,128)S(1)}, u32[]{:S(2)}, u32[]{:S(2)}) %collective-permute-start.4) | collective-permute-done | bytes 2080 | tf_op jit(solution)/shard_map/ppermute | solution.py:725
  18.7 1.7 %collective-permute-start.5 = (f32[8,64,1]{2,1,0:T(8,128)S(1)}, f32[8,64,1]{2,1,0:T(8,128)S(1)}, u32[]{:S(2)}, u32[]{:S(2)}) collective-permute-start(f32[8,64,1]{2,1,0:T(8,128)S(1)} %get-tuple-element.6), channel_id=1, source_target_pairs={{2,0},{4,2},{6,4},{0,6},{3,1},{5,3},{7,5},{1,7},{10,8},{12,10},{14... | collective-permute-start | bytes 6152 | tf_op jit(solution)/shard_map/ppermute | solution.py:726
  20.4 0.0 copy-start.1
  20.4 1.2 %copy-done.1 = f32[1,2,8,16,1024]{4,3,2,1,0:T(8,128)S(1)} copy-done((f32[1,2,8,16,1024]{4,3,2,1,0:T(8,128)S(1)}, f32[1,2,8,16,1024]{4,3,2,1,0:T(8,128)}, u32[]{:S(2)}) %copy-start.1) | copy-done | bytes 1048600
  21.6 0.0 copy-start.4
  21.6 0.9 copy-done.4
  22.6 0.0 copy-start.6
  22.6 0.8 copy-done.6
  23.3 37.6 %forward_lines.1.refs_10_ = f32[4,2,32,1152]{3,2,1,0:T(8,128)S(1)} custom-call(f32[2,8,16,1024]{3,2,1,0:T(8,128)S(1)} %bitcast.4, f32[2,32,128]{2,1,0:T(8,128)S(1)} %copy-done.6, bf16[128,768]{1,0:T(8,128)(2,1)S(1)} %copy-done.4), custom_call_target="tpu_custom_call" | custom-call | flops 1000000000 | bytes 100000000 | tf_op jit(solution)/shard_map/forward_lines/pallas_call | solution.py:309
  61.6 0.0 copy-start.2
  61.6 0.0 copy-start.3
  61.6 0.0 copy-start.5
  61.6 0.0 collective-permute-done.5.refs_9_
  61.7 0.0 collective-permute-done.2.refs_6_
  61.7 0.0 collective-permute-done.3.refs_7_
  61.7 0.0 collective-permute-done.refs_4_
  61.7 0.0 collective-permute-done.1.refs_5_
  61.7 0.0 copy-done
  61.7 26.5 %shard_map.104 = (f32[8,64,4096]{2,1,0:T(8,128)}, f32[2,16,1024]{2,1,0:T(8,128)S(1)}) custom-call(f32[8]{0:T(128)S(1)} %copy-done, f32[8,64,4096]{2,1,0:T(8,128)} %refs_3_.1, f32[8,64,4096]{2,1,0:T(8,128)} %refs_3_.1, f32[8,64,4096]{2,1,0:T(8,128)} %refs_3_.1, f32[1,64,4096]{2,1,0:T(8,128)S(1)} %collective-permute-done.refs_4_, ...), custom_call_target="tpu_custom_call" | custom-call | tf_op jit(solution)/shard_map/pallas_call | solution.py:665
  88.2 0.0 copy-done.2
  88.2 0.0 copy-done.3
  88.2 0.0 copy-done.5
  88.2 26.9 %backward_lines.1 = f32[2,8,16,1024]{3,2,1,0:T(8,128)S(1)} custom-call(f32[1]{0:T(128)S(6)} %copy.13.refs_0_, f32[2,16,1024]{2,1,0:T(8,128)S(1)} %get-tuple-element.5.refs_1_, f32[2,8,16,1024]{3,2,1,0:T(8,128)S(1)} %bitcast.5, f32[1,1024]{1,0:T(1,128)S(1)} %multiply_exponential_fusion.refs_3_, f32[2,32,128]{2,1,0:T(8,128)S(1)} %copy-done.5, ...), custom_call_target="tpu_custom_call" | custom-call | flops 1000000000 | bytes 50000000 | tf_op jit(solution)/shard_map/backward_lines/pallas_call | solution.py:494
  115.1 1.0 copy.14
  (8 shorter events, 0.1 us)
Async XLA Ops:
  0.6 61.1 %copy-start = (f32[8]{0:T(128)S(1)}, f32[8]{0:T(128)}, u32[]{:S(2)}) copy-start(f32[8]{0:T(128)} %refs_0_.2) | copy-start | bytes 100
  3.7 58.0 %collective-permute-start = (f32[1,64,4096]{2,1,0:T(8,128)}, f32[1,64,4096]{2,1,0:T(8,128)S(1)}, u32[]{:S(2)}, u32[]{:S(2)}) collective-permute-start(f32[1,64,4096]{2,1,0:T(8,128)} %get-tuple-element.11), channel_id=1, source_target_pairs={{0,8},{8,16},{16,24},{24,0},{1,9},{9,17},{17,25},{25,1},{2,10},{10... | collective-permute-start | bytes 3145736 | tf_op jit(solution)/shard_map/ppermute | solution.py:725
  6.7 55.0 %collective-permute-start.1 = (f32[1,64,4096]{2,1,0:T(8,128)}, f32[1,64,4096]{2,1,0:T(8,128)S(1)}, u32[]{:S(2)}, u32[]{:S(2)}) collective-permute-start(f32[1,64,4096]{2,1,0:T(8,128)} %get-tuple-element.10), channel_id=1, source_target_pairs={{8,0},{16,8},{24,16},{0,24},{9,1},{17,9},{25,17},{1,25},{10,2},{18... | collective-permute-start | bytes 3145736 | tf_op jit(solution)/shard_map/ppermute | solution.py:726
  8.8 9.9 %collective-permute-start.4 = (f32[8,64,1]{2,1,0:T(8,128)S(1)}, f32[8,64,1]{2,1,0:T(8,128)S(1)}, u32[]{:S(2)}, u32[]{:S(2)}) collective-permute-start(f32[8,64,1]{2,1,0:T(8,128)S(1)} %get-tuple-element.7), channel_id=1, source_target_pairs={{0,2},{2,4},{4,6},{6,0},{1,3},{3,5},{5,7},{7,1},{8,10},{10,12},{12... | collective-permute-start | bytes 6152 | tf_op jit(solution)/shard_map/ppermute | solution.py:725
  12.6 49.0 %collective-permute-start.2 = (f32[8,1,4096]{2,1,0:T(1,128)S(1)}, f32[8,1,4096]{2,1,0:T(1,128)S(1)}, u32[]{:S(2)}, u32[]{:S(2)}) collective-permute-start(f32[8,1,4096]{2,1,0:T(1,128)S(1)} %get-tuple-element.9), channel_id=1, source_target_pairs={{0,1},{1,0},{2,3},{3,2},{4,5},{5,4},{6,7},{7,6},{8,9},{9,8},{10,11... | collective-permute-start | bytes 393224 | tf_op jit(solution)/shard_map/ppermute | solution.py:725
  12.7 48.9 %collective-permute-start.3 = (f32[8,1,4096]{2,1,0:T(1,128)S(1)}, f32[8,1,4096]{2,1,0:T(1,128)S(1)}, u32[]{:S(2)}, u32[]{:S(2)}) collective-permute-start(f32[8,1,4096]{2,1,0:T(1,128)S(1)} %get-tuple-element.8), channel_id=1, source_target_pairs={{1,0},{0,1},{3,2},{2,3},{5,4},{4,5},{7,6},{6,7},{9,8},{8,9},{11,10... | collective-permute-start | bytes 393224 | tf_op jit(solution)/shard_map/ppermute | solution.py:726
  18.7 43.0 %collective-permute-start.5 = (f32[8,64,1]{2,1,0:T(8,128)S(1)}, f32[8,64,1]{2,1,0:T(8,128)S(1)}, u32[]{:S(2)}, u32[]{:S(2)}) collective-permute-start(f32[8,64,1]{2,1,0:T(8,128)S(1)} %get-tuple-element.6), channel_id=1, source_target_pairs={{2,0},{4,2},{6,4},{0,6},{3,1},{5,3},{7,5},{1,7},{10,8},{12,10},{14... | collective-permute-start | bytes 6152 | tf_op jit(solution)/shard_map/ppermute | solution.py:726
  20.4 1.2 %copy-start.1 = (f32[1,2,8,16,1024]{4,3,2,1,0:T(8,128)S(1)}, f32[1,2,8,16,1024]{4,3,2,1,0:T(8,128)}, u32[]{:S(2)}) copy-start(f32[1,2,8,16,1024]{4,3,2,1,0:T(8,128)} %param.9) | copy-start | bytes 3145732
  21.6 0.9 copy-start.4
  22.6 0.8 copy-start.6
  61.6 26.6 %copy-start.2 = (f32[1,2,8,16,1024]{4,3,2,1,0:T(8,128)S(1)}, f32[1,2,8,16,1024]{4,3,2,1,0:T(8,128)}, u32[]{:S(2)}) copy-start(f32[1,2,8,16,1024]{4,3,2,1,0:T(8,128)} %param.9) | copy-start | bytes 3145732
  61.6 26.6 %copy-start.3 = (bf16[256,768]{1,0:T(8,128)(2,1)S(1)}, bf16[256,768]{1,0:T(8,128)(2,1)}, u32[]{:S(2)}) copy-start(bf16[256,768]{1,0:T(8,128)(2,1)} %constant.141.clone.refs_5_) | copy-start | bytes 1179652
  61.6 26.6 %copy-start.5 = (f32[2,32,128]{2,1,0:T(8,128)S(1)}, f32[2,32,128]{2,1,0:T(8,128)}, u32[]{:S(2)}) copy-start(f32[2,32,128]{2,1,0:T(8,128)} %constant.140.clone.refs_4_) | copy-start | bytes 98308

commit v2 on v1

--- a/solution.py
+++ b/solution.py
@@ -155,9 +155,15 @@
     columns,
     halves_y,
     modes_ref,
-    twist_ref,
-    table_ref,
+    cells_ref,
+    twist_hbm,
+    table_hbm,
     rim_ref,
+    heat_ref,
+    edge_ref,
+    south_ref,
+    north_ref,
+    outer_ref,
     pencil,
     mid,
     turn,
@@ -165,6 +171,14 @@
     landed,
     side_out,
     side_in,
+    twist_ref,
+    table_ref,
+    edge_rows,
+    edge_cols,
+    row_out,
+    row_in,
+    col_out,
+    col_in,
     send_one,
     recv_one,
     own_sem,
@@ -172,6 +186,13 @@
     recv_two,
     side_send,
     side_recv,
+    load_sem,
+    row_send,
+    row_recv,
+    col_send,
+    col_recv,
+    outer_send,
+    outer_recv,
 ):
     mine, at, half = lax.axis_index("grp"), lax.axis_index("gx"), lax.axis_index("gy")
     above, below = lax.rem(half + 1, halves_y), lax.rem(half + halves_y - 1, halves_y)
@@ -182,6 +203,22 @@
     turns = pencil.shape[0]
     count = pencil.shape[3] // LANES
     span = width + LANES
+    levels, fine_rows, fine_cols = cells_ref.shape
+    loads = [
+        pltpu.make_async_copy(source, target, load_sem.at[k])
+        for k, (source, target) in enumerate(
+            (
+                (cells_ref.at[:, pl.ds(fine_rows - SUBLANES, SUBLANES), :], edge_rows.at[0]),
+                (cells_ref.at[:, pl.ds(0, SUBLANES), :], edge_rows.at[1]),
+                (cells_ref.at[:, :, pl.ds(fine_cols - LANES, LANES)], edge_cols.at[0]),
+                (cells_ref.at[:, :, pl.ds(0, LANES)], edge_cols.at[1]),
+                (twist_hbm, twist_ref),
+                (table_hbm, table_ref),
+            )
+        )
+    ]
+    for load in loads:
+        load.start()
     greet(groups, columns, (above, below))
 
     def place(block):
@@ -206,9 +243,70 @@
             device_id_type=MESH,
         )
 
+    def outer_copies(piece):
+        row = pl.ds(piece * SUBLANES, SUBLANES)
+        return [
+            pltpu.make_async_remote_copy(
+                src_ref=cells_ref.at[(levels - 1, 0)[k], row, :],
+                dst_ref=outer_ref.at[k, row, :],
+                send_sem=outer_send.at[k, piece],
+                recv_sem=outer_recv.at[k, piece],
+                device_id={"grp": lax.rem(mine + (1, groups - 1)[k], groups)},
+                device_id_type=MESH,
+            )
+            for k in range(2)
+        ]
+
+    pieces = fine_rows // SUBLANES
+    ahead = min(4, pieces)
+    during = min(turns, pieces - ahead)
+
+    def start_outer(piece):
+        for copy in outer_copies(piece):
+            copy.start()
+
     for i in range(turns):
         for d in range(columns):
             first_copy(i, (d + 1) % columns).start()
+    for piece in range(ahead):
+        start_outer(piece)
+
+    for load in loads:
+        load.wait()
+    lane_at = lax.broadcasted_iota(jnp.int32, (fine_rows, LANES), 1)
+    for level in range(levels):
+        row_out[0, level : level + 1, :] = edge_rows[0, level, SUBLANES - 1 : SUBLANES, :]
+        row_out[1, level : level + 1, :] = edge_rows[1, level, 0:1, :]
+    for k in range(2):
+        packed = jnp.zeros((fine_rows, LANES), jnp.float32)
+        for level in range(levels):
+            column = edge_cols[k, level, :, LANES - 1 : LANES] if k == 0 else edge_cols[k, level, :, 0:1]
+            packed = jnp.where(lane_at == level, column, packed)
+        col_out[k] = packed
+    outer = []
+    for k in range(2):
+        outer.append(
+            pltpu.make_async_remote_copy(
+                src_ref=row_out.at[k],
+                dst_ref=row_in.at[k],
+                send_sem=row_send.at[k],
+                recv_sem=row_recv.at[k],
+                device_id={"gy": (above, below)[k]},
+                device_id_type=MESH,
+            )
+        )
+        outer.append(
+            pltpu.make_async_remote_copy(
+                src_ref=col_out.at[k],
+                dst_ref=col_in.at[k],
+                send_sem=col_send.at[k],
+                recv_sem=col_recv.at[k],
+                device_id={"gx": lax.rem(at + (1, columns - 1)[k], columns)},
+                device_id_type=MESH,
+            )
+        )
+    for copy in outer:
+        copy.start()
 
     def second_copy(i, b):
         group, inner, plane, row = place(at + columns * i)
@@ -245,9 +343,15 @@
             remote, local, stays = second_copy(i, b)
             pl.when(stays)(lambda: local().start())
             pl.when(jnp.logical_not(stays))(lambda: remote().start())
+        if during == turns:
+            start_outer(ahead + i)
+        else:
+            pl.when(i < during)(lambda: start_outer(ahead + i))
         return carry
 
     lax.fori_loop(0, turns, one_turn, 0)
+    for piece in range(ahead + during, pieces):
+        start_outer(piece)
     for field in range(groups):
         for inner in range(blocks):
             plane, row = inner // row_blocks, inner % row_blocks * SUBLANES
@@ -271,20 +375,48 @@
     ]
     for side in sides:
         side.start()
-    for field in range(groups):
+    scale = fine_step * 0.5
+    for field in range(groups - 1):
         for plane in range(quarter):
-            rim_ref[field, plane, 0:rows, :] = landed[field, plane]
+            rim_ref[field, plane, 0:rows, :] = scale * landed[field, plane]
+    for copy in outer:
+        copy.wait()
+    for level in range(levels):
+        south_ref[level] = row_in[0, level : level + 1, :]
+        north_ref[level] = row_in[1, level : level + 1, :]
+        edge_ref[level] = jnp.where(
+            lane_at < LANES // 2,
+            col_in[1, :, level : level + 1],
+            col_in[0, :, level : level + 1],
+        )
     for side in sides:
         side.wait()
     rest = rim_ref.shape[2] - rows - 2
-    for field in range(groups):
+    for field in range(groups - 1):
         for plane in range(quarter):
             k = field * quarter + plane
             tail = jnp.concatenate(
-                [side_in[0, k : k + 1, :], side_in[1, k : k + 1, :], jnp.zeros((rest, span), jnp.float32)],
+                [
+                    scale * side_in[0, k : k + 1, :],
+                    scale * side_in[1, k : k + 1, :],
+                    jnp.zeros((rest, span), jnp.float32),
+                ],
                 axis=0,
             )
             rim_ref[field, plane, rows:, :] = tail
+    near, far = mean_weights()
+    row_at = lax.broadcasted_iota(jnp.int32, (rows, span), 0)
+    for plane in range(quarter):
+        k = (groups - 1) * quarter + plane
+        heat = landed[groups - 1, plane]
+        before = jnp.where(row_at == 0, side_in[0, k : k + 1, :], pltpu.roll(heat, 1, 0))
+        after = jnp.where(row_at == rows - 1, side_in[1, k : k + 1, :], pltpu.roll(heat, rows - 1, 0))
+        heat = near * heat + far * (before + after)
+        heat = near * pltpu.roll(heat, span - 1, 1) + far * (heat + pltpu.roll(heat, span - 2, 1))
+        heat_ref[plane] = heat[:, :width]
+    for piece in range(pieces):
+        for copy in outer_copies(piece):
+            copy.wait()
     for i in range(turns):
         for d in range(1, columns):
             first_copy(i, d).wait_send()
@@ -293,8 +425,15 @@
             pl.when(jnp.logical_not(stays))(lambda: remote().wait_send())
 
 
-def forward(modes, groups, columns, halves_y):
+def mean_weights():
+    offsets = [(s + 0.5) / RATIO - 0.5 for s in range(RATIO)]
+    near = sum(1.0 - abs(offset) for offset in offsets) / RATIO
+    return near, (1.0 - near) / 2.0
+
+
+def forward(modes, cells, groups, columns, halves_y):
     _, planes, rows, width = modes.shape
+    levels, fine_rows, fine_cols = cells.shape
     length = width * columns
     quarter = planes // groups
     blocks = quarter * (rows // SUBLANES)
@@ -309,9 +448,16 @@
     return pl.pallas_call(
         lambda *refs: forward_kernel(groups, columns, halves_y, *refs),
         name="forward_lines",
-        out_shape=jax.ShapeDtypeStruct((groups, quarter, deep, span), jnp.float32),
-        in_specs=[vmem] * 3,
-        out_specs=vmem,
+        out_shape=[
+            jax.ShapeDtypeStruct((groups - 1, quarter, deep, span), jnp.float32),
+            jax.ShapeDtypeStruct((quarter, rows, width), jnp.float32),
+            jax.ShapeDtypeStruct((levels, fine_rows, LANES), jnp.float32),
+            jax.ShapeDtypeStruct((levels, 1, fine_cols), jnp.float32),
+            jax.ShapeDtypeStruct((levels, 1, fine_cols), jnp.float32),
+            jax.ShapeDtypeStruct((2, fine_rows, fine_cols), jnp.float32),
+        ],
+        in_specs=[pl.BlockSpec(memory_space=pltpu.HBM)] * 4,
+        out_specs=[vmem] * 5 + [pl.BlockSpec(memory_space=pltpu.HBM)],
         scratch_shapes=[
             pltpu.VMEM((turns, 2, SUBLANES, length), jnp.float32),
             pltpu.VMEM((2, SUBLANES * count, LANES), jnp.float32),
@@ -320,6 +466,14 @@
             pltpu.VMEM((groups, quarter, rows, span), jnp.float32),
             pltpu.VMEM((2, groups * quarter, span), jnp.float32),
             pltpu.VMEM((2, groups * quarter, span), jnp.float32),
+            pltpu.VMEM(twist.shape, jnp.float32),
+            pltpu.VMEM(table.shape, jnp.bfloat16),
+            pltpu.VMEM((2, levels, SUBLANES, fine_cols), jnp.float32),
+            pltpu.VMEM((2, levels, fine_rows, LANES), jnp.float32),
+            pltpu.VMEM((2, levels, fine_cols), jnp.float32),
+            pltpu.VMEM((2, levels, fine_cols), jnp.float32),
+            pltpu.VMEM((2, fine_rows, LANES), jnp.float32),
+            pltpu.VMEM((2, fine_rows, LANES), jnp.float32),
             dma((turns, columns)),
             dma((turns, columns)),
             dma((turns,)),
@@ -327,12 +481,19 @@
             dma((groups, blocks)),
             dma((2,)),
             dma((2,)),
+            dma((6,)),
+            dma((2,)),
+            dma((2,)),
+            dma((2,)),
+            dma((2,)),
+            dma((2, fine_rows // SUBLANES)),
+            dma((2, fine_rows // SUBLANES)),
         ],
         compiler_params=pltpu.CompilerParams(
-            collective_id=0, has_side_effects=True, vmem_limit_bytes=32 * 2**20
+            collective_id=0, has_side_effects=True, vmem_limit_bytes=63 * 2**20
         ),
         cost_estimate=pl.CostEstimate(flops=10**9, bytes_accessed=10**8, transcendentals=0),
-    )(modes, twist, table)
+    )(modes, cells, twist, table)
 
 
 def backward_kernel(
@@ -516,38 +677,35 @@
     )(gain, cells, modes, damping, twist, table)
 
 
-def spread_table(cell_count, source_count):
-    fine_count = cell_count * RATIO
-    source = lax.broadcasted_iota(jnp.int32, (source_count, fine_count), 0)
-    fine_cell = lax.broadcasted_iota(jnp.int32, (source_count, fine_count), 1)
+def rows_table(row_count, source_count):
+    fine_row = np.arange(row_count * RATIO)
+    parent = fine_row // RATIO
+    offset = (fine_row % RATIO + 0.5) / RATIO - 0.5
+    table = np.zeros((row_count * RATIO, source_count), np.float32)
+    beside = np.where(
+        offset > 0,
+        np.where(parent == row_count - 1, row_count + 1, parent + 1),
+        np.where(parent == 0, row_count, parent - 1),
+    )
+    table[fine_row, parent] = 1.0 - np.abs(offset)
+    table[fine_row, beside] = np.abs(offset)
+    return np.concatenate([table, table], axis=1).astype(jnp.bfloat16)
+
+
+def lanes_table(cell_count):
+    fine_cell = np.arange(cell_count * RATIO)
     parent = fine_cell // RATIO
-    sub_cell = (fine_cell % RATIO).astype(jnp.float32)
-    offset = (sub_cell + 0.5) / RATIO - 0.5
-    magnitude = jnp.abs(offset)
-    own_weight = jnp.where(source == parent + 1, 1.0 - magnitude, 0.0)
-    after_weight = jnp.where((source == parent + 2) & (offset > 0), magnitude, 0.0)
-    before_weight = jnp.where((source == parent) & (offset < 0), magnitude, 0.0)
-    return (own_weight + after_weight + before_weight).astype(jnp.bfloat16)
-
-
-def rows_table(row_count, source_count):
-    source = lax.broadcasted_iota(jnp.int32, (row_count * RATIO, source_count), 1)
-    fine_row = lax.broadcasted_iota(jnp.int32, (row_count * RATIO, source_count), 0)
-    parent = fine_row // RATIO
-    offset = ((fine_row % RATIO).astype(jnp.float32) + 0.5) / RATIO - 0.5
-    magnitude = jnp.abs(offset)
-    before = jnp.where(parent == 0, row_count, parent - 1)
-    after = jnp.where(parent == row_count - 1, row_count + 1, parent + 1)
-    own_weight = jnp.where(source == parent, 1.0 - magnitude, 0.0)
-    after_weight = jnp.where((source == after) & (offset > 0), magnitude, 0.0)
-    before_weight = jnp.where((source == before) & (offset < 0), magnitude, 0.0)
-    return (own_weight + after_weight + before_weight).astype(jnp.bfloat16)
+    offset = (fine_cell % RATIO + 0.5) / RATIO - 0.5
+    table = np.zeros((LANES, cell_count * RATIO), np.float32)
+    table[parent + 1, fine_cell] = 1.0 - np.abs(offset)
+    table[np.where(offset > 0, parent + 2, parent), fine_cell] = np.abs(offset)
+    return np.concatenate([table, table], axis=0).astype(jnp.bfloat16)
 
 
 def average_table(fine_count, weight):
-    fine_cell = lax.broadcasted_iota(jnp.int32, (fine_count, fine_count // RATIO), 0)
-    coarse_cell = lax.broadcasted_iota(jnp.int32, (fine_count, fine_count // RATIO), 1)
-    return jnp.where(fine_cell // RATIO == coarse_cell, weight, 0.0).astype(jnp.bfloat16)
+    cell = np.arange(fine_count // RATIO)[None, :]
+    table = np.where(np.arange(fine_count)[:, None] // RATIO == cell, weight, 0.0)
+    return np.concatenate([table, table], axis=0).astype(jnp.bfloat16)
 
 
 def split_parts(value):
@@ -559,184 +717,239 @@
     return jnp.dot(left, right, preferred_element_type=jnp.float32)
 
 
-def step_kernel(
-    cells_coarse,
-    diff_ref,
-    centre_ref,
-    below_ref,
-    above_ref,
-    lower_ref,
-    upper_ref,
+def split_pair(value, axis):
+    return jnp.concatenate(split_parts(value), axis=axis)
+
+
+def block_means(total, rows_ref, lanes_ref):
+    half = product(rows_ref[...], split_pair(total, 0))
+    fine = LANES * RATIO
+    chunks = half.shape[1] // fine
+    stacked = jnp.concatenate([half[:, k * fine : (k + 1) * fine] for k in range(chunks)], axis=0)
+    cells = product(split_pair(stacked, 1), lanes_ref[...])
+    height = half.shape[0]
+    return [cells[k * height : (k + 1) * height] for k in range(chunks)]
+
+
+def fine_kernel(
+    rate_ref,
+    cells_hbm,
+    edge_ref,
     south_ref,
     north_ref,
-    west_ref,
-    east_ref,
+    beyond_hbm,
     rim_ref,
+    heat_ref,
     ty_ref,
     tx_ref,
     ry_ref,
     rx_ref,
-    out_ref,
+    out_hbm,
     coarse_ref,
-    vel_ref,
-    acc_ref,
+    held,
+    vel,
+    acc,
+    ready,
+    in_sem,
+    out_sem,
 ):
-    level = pl.program_id(0)
-    last = pl.num_programs(0) - 1
-    part = lax.rem(level, RATIO)
-    rows, cols = centre_ref.shape[1], centre_ref.shape[2]
-    fine = cells_coarse * RATIO
-    chunks = cols // fine
-    span = tx_ref.shape[0]
-
-    @pl.when(part == 0)
+    plane = pl.program_id(0)
+    slabs, spans, tall = held.shape[:3]
+    levels, rows, cols = cells_hbm.shape
+    strips, tiles = rows // SUBLANES, cols // LANES
+    fields = rim_ref.shape[0]
+    pieces = vel.shape[0]
+    half = LANES // 2
+
+    def load(source, index, tile, slab):
+        return pltpu.make_async_copy(
+            source.at[index, :, pl.ds(pl.multiple_of(tile * LANES, LANES), LANES)],
+            held.at[slab, tile, pl.ds(SUBLANES, rows), :],
+            in_sem.at[slab],
+        )
+
+    def start_slab(source, index, slab):
+        @pl.loop(0, tiles)
+        def _(tile):
+            load(source, index, tile, slab).start()
+
+    def wait_slab(slab):
+        whole = held.at[slab, pl.ds(0, tiles), pl.ds(SUBLANES, rows), :]
+        pltpu.make_async_copy(whole, whole, in_sem.at[slab]).wait()
+
+    @pl.when(plane == 0)
     def _():
-        for field in range(rim_ref.shape[0]):
-            high, low = split_parts(rim_ref[field, 0])
-            along = product(ty_ref[...], high) + product(ty_ref[...], low)
-            high, low = split_parts(along)
-            for k in range(chunks):
-                window = slice(k * cells_coarse, k * cells_coarse + span)
-                vel_ref[field, :, k * fine : (k + 1) * fine] = product(
-                    high[:, window], tx_ref[...]
-                ) + product(low[:, window], tx_ref[...])
-        acc_ref[...] = jnp.zeros_like(acc_ref)
-
-    rate = diff_ref[level]
-    row_at = lax.broadcasted_iota(jnp.int32, (rows, fine), 0)
-    lane_at = lax.broadcasted_iota(jnp.int32, (rows, fine), 1)
-    first_lane, last_lane = lane_at == 0, lane_at == fine - 1
-    first_row, last_row = row_at == 0, row_at == rows - 1
-    bottom, top = level == 0, level == last
-    for k in range(chunks):
-        start, stop = k * fine, (k + 1) * fine
-        centre = centre_ref[0, :, start:stop]
-        before = west_ref[0] if k == 0 else centre_ref[0, :, start - 1 : start]
-        after = east_ref[0] if k == chunks - 1 else centre_ref[0, :, stop : stop + 1]
-        west = jnp.where(first_lane, before, pltpu.roll(centre, 1, 1))
-        east = jnp.where(last_lane, after, pltpu.roll(centre, fine - 1, 1))
-        south = jnp.where(first_row, south_ref[0, :, start:stop], pltpu.roll(centre, 1, 0))
-        north = jnp.where(
-            last_row, north_ref[0, :, start:stop], pltpu.roll(centre, rows - 1, 0)
-        )
-        lower = jnp.where(bottom, lower_ref[0, :, start:stop], below_ref[0, :, start:stop])
-        upper = jnp.where(top, upper_ref[0, :, start:stop], above_ref[0, :, start:stop])
-        spread = rate * (east + west + north + south + upper + lower - 6.0 * centre)
-        advection = (
-            vel_ref[0, :, start:stop] * (east - west)
-            + vel_ref[1, :, start:stop] * (north - south)
-            + vel_ref[2, :, start:stop] * (upper - lower)
-        ) * 0.5
-        updated = centre + fine_step * (spread - advection)
-        out_ref[0, :, start:stop] = updated
-        acc_ref[:, start:stop] += vel_ref[3, :, start:stop] - updated
-
-    @pl.when(part == RATIO - 1)
+        start_slab(beyond_hbm, 0, 0)
+
+        @pl.loop(0, levels)
+        def _(level):
+            start_slab(cells_hbm, level, level + 1)
+
+        start_slab(beyond_hbm, 1, slabs - 1)
+
+    for part in range(RATIO):
+        level = plane * RATIO + part
+        held[level + 1, tiles, SUBLANES : SUBLANES + rows, :] = edge_ref[part]
+        for tile in range(tiles):
+            lanes = slice(tile * LANES, (tile + 1) * LANES)
+            held[level + 1, tile, SUBLANES - 1 : SUBLANES, :] = south_ref[part, :, lanes]
+            held[level + 1, tile, SUBLANES + rows : SUBLANES + rows + 1, :] = north_ref[part, :, lanes]
+
+    along = jnp.concatenate(
+        [product(ty_ref[...], split_pair(rim_ref[field, 0], 0)) for field in range(fields)],
+        axis=0,
+    )
+    span = along.shape[1]
+    views = [split_parts(along), split_parts(pltpu.roll(along, span - half, 1))]
+    group = min(4, pieces)
+    for first in range(0, pieces, group):
+        windows = []
+        for k in range(first, first + group):
+            high, low = views[k % 2]
+            lanes = slice(k // 2 * LANES, (k // 2 + 1) * LANES)
+            windows.append(jnp.concatenate([high[:, lanes], low[:, lanes]], axis=1))
+        refined = product(jnp.concatenate(windows, axis=0), tx_ref[...])
+        for k in range(group):
+            vel[first + k] = refined[k * fields * rows : (k + 1) * fields * rows]
+
+    @pl.when(plane == 0)
     def _():
-        for k in range(chunks):
-            high, low = split_parts(acc_ref[:, k * fine : (k + 1) * fine])
-            half = product(ry_ref[...], high) + product(ry_ref[...], low)
-            high, low = split_parts(half)
-            coarse_ref[0, :, k * cells_coarse : (k + 1) * cells_coarse] = product(
-                high, rx_ref[...]
-            ) + product(low, rx_ref[...])
-
-
-def fine_update(rimmed, salinity, halos, diffusivity):
+        wait_slab(0)
+        wait_slab(1)
+
+    for part in range(RATIO):
+        wait_slab(plane * RATIO + part + 2)
+
+    side_rates = [fine_step * rate_ref[plane * RATIO + part] for part in range(RATIO)]
+    own_rates = [1.0 - 6.0 * rate for rate in side_rates]
+    lane_at = lax.broadcasted_iota(jnp.int32, (SUBLANES, LANES), 1)
+    first_lane, last_lane = lane_at == 0, lane_at == LANES - 1
+    per_turn = vel.shape[2] // LANES
+    base = plane * RATIO
+
+    def out_copy(index, strip):
+        at = pl.ds(pl.multiple_of(strip * SUBLANES, SUBLANES), SUBLANES)
+        block = pl.ds(index * RATIO, RATIO)
+        return pltpu.make_async_copy(
+            ready.at[block, at, :], out_hbm.at[block, at, :], out_sem.at[index, strip]
+        )
+
+    @pl.loop(0, strips)
+    def _(s):
+        start = pl.multiple_of(s * SUBLANES, SUBLANES)
+        at = pl.ds(start, SUBLANES)
+        middle = pl.ds(start + SUBLANES, SUBLANES)
+        below, above = pl.ds(start + SUBLANES - 1, SUBLANES), pl.ds(start + SUBLANES + 1, SUBLANES)
+        slabs_here = [base + part + 1 for part in range(RATIO)]
+        west_turned = [pltpu.roll(held[slab, tiles, middle, :], 1, 1) for slab in slabs_here]
+        centre = [held[slab, 0, middle, :] for slab in slabs_here]
+        east_turned = [pltpu.roll(x, LANES - 1, 1) for x in centre]
+        for tile in range(tiles):
+            k, j = divmod(tile, per_turn)
+            lanes = slice(tile * LANES, (tile + 1) * LANES)
+            inner = slice(j * LANES, (j + 1) * LANES)
+            ahead = [held[slab, tile + 1, middle, :] for slab in slabs_here]
+            ahead_turned = [pltpu.roll(x, LANES - 1, 1) for x in ahead]
+            here_turned = [pltpu.roll(x, 1, 1) for x in centre]
+            column = (
+                [held[base, tile, middle, :]] + centre + [held[base + RATIO + 1, tile, middle, :]]
+            )
+            flow = [
+                vel[k, pl.ds(pl.multiple_of(f * rows + start, SUBLANES), SUBLANES), inner]
+                for f in range(fields)
+            ]
+            total = None
+            for part, slab in enumerate(slabs_here):
+                west = jnp.where(first_lane, west_turned[part], here_turned[part])
+                east = jnp.where(last_lane, ahead_turned[part], east_turned[part])
+                south, north = held[slab, tile, below, :], held[slab, tile, above, :]
+                lower, upper = column[part], column[part + 2]
+                around = (east + west) + (north + south) + (upper + lower)
+                advection = (
+                    flow[0] * (east - west)
+                    + flow[1] * (north - south)
+                    + flow[2] * (upper - lower)
+                )
+                updated = own_rates[part] * centre[part] + side_rates[part] * around - advection
+                ready[base + part, at, lanes] = updated
+                total = updated if total is None else total + updated
+            acc[at, lanes] = total
+            west_turned, centre, east_turned = here_turned, ahead, ahead_turned
+        out_copy(plane, s).start()
+
+    for k, cells in enumerate(block_means(acc[...], ry_ref, rx_ref)):
+        lanes = slice(k * LANES, (k + 1) * LANES)
+        coarse_ref[0, :, lanes] = heat_ref[0, :, lanes] - cells
+
+    @pl.when(plane == pl.num_programs(0) - 1)
+    def _():
+        for index in range(levels // RATIO):
+            for s in range(strips):
+                out_copy(index, s).wait()
+
+
+def fine_update(rimmed, heat, edge, south, north, beyond, salinity, diffusivity):
     levels, rows, cols = salinity.shape
-    fields, quarter, rim_rows, rim_cols = rimmed.shape
+    fields, quarter = rimmed.shape[:2]
     row_count, width = rows // RATIO, cols // RATIO
-    cells_coarse = min(128, width)
-    fine = cells_coarse * RATIO
-    span = cells_coarse + 128
-    ty = rows_table(row_count, rim_rows)
-    tx = spread_table(cells_coarse, span)
+    cell_count = LANES // 2
+    ty = rows_table(row_count, rimmed.shape[2])
+    tx = lanes_table(cell_count)
     ry = average_table(rows, 1.0 / RATIO).T
-    rx = average_table(fine, 1.0 / RATIO / RATIO)
+    rx = average_table(LANES * RATIO, 1.0 / RATIO / RATIO)
+    pieces = width // cell_count
 
     def fixed(array):
         return pl.BlockSpec(array.shape, lambda i: (0,) * array.ndim)
 
-    def level_block(array):
-        return pl.BlockSpec((1,) + array.shape[1:], lambda i: (i, 0, 0))
-
-    slab = (1, rows, cols)
-    lower, upper, south, north, west, east = halos
+    hbm = pl.BlockSpec(memory_space=pltpu.HBM)
     return pl.pallas_call(
-        lambda *refs: step_kernel(cells_coarse, *refs),
-        grid=(levels,),
+        fine_kernel,
+        name="fine_levels",
+        grid=(quarter,),
         in_specs=[
             pl.BlockSpec(memory_space=pltpu.SMEM),
-            pl.BlockSpec(slab, lambda i: (i, 0, 0)),
-            pl.BlockSpec(slab, lambda i: (jnp.maximum(i - 1, 0), 0, 0)),
-            pl.BlockSpec(slab, lambda i: (jnp.minimum(i + 1, levels - 1), 0, 0)),
-            fixed(lower),
-            fixed(upper),
-            level_block(south),
-            level_block(north),
-            level_block(west),
-            level_block(east),
-            pl.BlockSpec((fields, 1) + rimmed.shape[2:], lambda i: (0, i // RATIO, 0, 0)),
+            hbm,
+            pl.BlockSpec((RATIO, rows, LANES), lambda i: (i, 0, 0)),
+            pl.BlockSpec((RATIO, 1, cols), lambda i: (i, 0, 0)),
+            pl.BlockSpec((RATIO, 1, cols), lambda i: (i, 0, 0)),
+            hbm,
+            pl.BlockSpec((fields, 1) + rimmed.shape[2:], lambda i: (0, i, 0, 0)),
+            pl.BlockSpec((1, row_count, width), lambda i: (i, 0, 0)),
             fixed(ty),
             fixed(tx),
             fixed(ry),
             fixed(rx),
         ],
-        out_specs=[
-            pl.BlockSpec(slab, lambda i: (i, 0, 0)),
-            pl.BlockSpec((1, row_count, width), lambda i: (i // RATIO, 0, 0)),
-        ],
+        out_specs=[hbm, pl.BlockSpec((1, row_count, width), lambda i: (i, 0, 0))],
         out_shape=[
             jax.ShapeDtypeStruct(salinity.shape, jnp.float32),
             jax.ShapeDtypeStruct((quarter, row_count, width), jnp.float32),
         ],
         scratch_shapes=[
-            pltpu.VMEM((fields, rows, cols), jnp.float32),
+            pltpu.VMEM((levels + 2, cols // LANES + 1, rows + 2 * SUBLANES, LANES), jnp.float32),
+            pltpu.VMEM((pieces, fields * rows, cell_count * RATIO), jnp.float32),
             pltpu.VMEM((rows, cols), jnp.float32),
+            pltpu.VMEM((levels, rows, cols), jnp.float32),
+            pltpu.SemaphoreType.DMA((levels + 2,)),
+            pltpu.SemaphoreType.DMA((quarter, rows // SUBLANES)),
         ],
         compiler_params=pltpu.CompilerParams(
-            dimension_semantics=("arbitrary",), vmem_limit_bytes=48 * 2**20
+            dimension_semantics=("arbitrary",), vmem_limit_bytes=63 * 2**20
         ),
-    )(
-        diffusivity,
-        salinity,
-        salinity,
-        salinity,
-        lower,
-        upper,
-        south,
-        north,
-        west,
-        east,
-        rimmed,
-        ty,
-        tx,
-        ry,
-        rx,
-    )
-
-
-def side_layers(cells, axis, dim):
-    count = lax.axis_size(axis)
-    extent = cells.shape[dim]
-    head = lax.slice_in_dim(cells, 0, 1, axis=dim)
-    tail = lax.slice_in_dim(cells, extent - 1, extent, axis=dim)
-    return (
-        lax.ppermute(tail, axis, [(i, (i + 1) % count) for i in range(count)]),
-        lax.ppermute(head, axis, [((i + 1) % count, i) for i in range(count)]),
-    )
+        cost_estimate=pl.CostEstimate(flops=10**9, bytes_accessed=4 * 10**7, transcendentals=0),
+    )(diffusivity, salinity, edge, south, north, beyond, rimmed, heat, ty, tx, ry, rx)
 
 
 def per_device(coarse_modes, salinity, viscosity, forcing_gain, diffusivity):
     width = coarse_modes.shape[4]
     groups, columns = lax.axis_size("grp"), lax.axis_size("gx")
-    halos = (
-        side_layers(salinity, "grp", 0)
-        + side_layers(salinity, "gy", 1)
-        + side_layers(salinity, "gx", 2)
+    rimmed, heat, edge, south, north, beyond = forward(
+        coarse_modes[0], salinity, groups, columns, lax.axis_size("gy")
     )
-    rimmed = forward(coarse_modes[0], groups, columns, lax.axis_size("gy"))
-    salinity_next, restricted = fine_update(rimmed, salinity, halos, diffusivity)
+    salinity_next, restricted = fine_update(
+        rimmed, heat, edge, south, north, beyond, salinity, diffusivity
+    )
     total_modes = width * columns
     mode_index = lax.axis_index("gx") * width + lax.broadcasted_iota(jnp.int32, (1, width), 1)
     wavenumber = jnp.where(mode_index < total_modes // 2, mode_index, mode_index - total_modes)

time: 118 us -> 104 us (0.88); the launches traced: 116 us -> 104 us
  starting transfers between devices: 8.34 us -> 0 us
  Pallas kernels: 91 us -> 98.5 us
  local copies, waits for them, and re-layouts: 9.86 us -> 3.11 us
  waiting for transfers between devices: 4.06 us -> 0 us
    pallas_call x1, Pallas kernels: 37.6 us -> 62 us  [forward(): pl.pallas_call(lambda *refs: forward_kernel(groups, columns, halves_y, *r...]
    pallas_call x1, Pallas kernels: 26.5 us -> 15.3 us  [fine_update(): pl.pallas_call(fine_kernel, name='fine_levels', grid=(quarter,), in_specs...]
    ppermute x6 -> x0, starting transfers between devices: 8.34 us -> none  [the longest x3 5.14 us: side_layers(): lax.ppermute(tail, axis, [(i, (i + 1) % count) for i in range(count)])]
    slice x3 -> x0, local copies, waits for them, and re-layouts: 5.96 us -> none  [side_layers(): head = lax.slice_in_dim(cells, 0, 1, axis=dim)]
    pallas_call x1, Pallas kernels: 26.9 us -> 21.2 us  [backward(): pl.pallas_call(lambda *refs: backward_kernel(groups, columns, *refs), nam...]
    ppermute x6 -> x0, waiting for transfers between devices: 4.06 us -> none  [the longest x3 4.06 us: side_layers(): lax.ppermute(tail, axis, [(i, (i + 1) % count) for i in range(count)])]
    unnamed x15 -> x9, local copies, waits for them, and re-layouts: 3.9 us -> 3.11 us
  transfers between devices with their start and end apart: 6 -> 0, of which waited for: 1 -> 0; matrix products, arithmetic and copies ran while one was open for 3% -> 0% of each run, Pallas kernels for 32% -> 0%
where the time goes in v2:
time: 104 us
  Pallas kernels  98.5 us (95%)
  local copies, waits for them, and re-layouts  3.11 us (3%)
  between operations  2 us (2%)
    pallas_call x1, Pallas kernels, forward(): pl.pallas_call(lambda *refs: forward_kernel(groups, columns, halves_y, *r...  62 us
    pallas_call x1, Pallas kernels, backward(): pl.pallas_call(lambda *refs: backward_kernel(groups, columns, *refs), nam...  21.2 us
    pallas_call x1, Pallas kernels, fine_update(): pl.pallas_call(fine_kernel, name='fine_levels', grid=(quarter,), in_specs...  15.3 us
    unnamed x9, local copies, waits for them, and re-layouts  3.11 us

profile of v2, /device:TPU:0, one launch (start us, length us, event | category | flops | bytes accessed | tf_op | source)
XLA Modules:
  0.0 103.6 jit_solution(5609674283739792281)
XLA Ops:
  0.6 62.0 %forward_lines.1 = (f32[3,2,32,1152]{3,2,1,0:T(8,128)}, f32[2,16,1024]{2,1,0:T(8,128)}, f32[8,64,128]{2,1,0:T(8,128)}, f32[8,1,4096]{2,1,0:T(1,128)}, f32[8,1,4096]{2,1,0:T(1,128)}, /*index=5*/f32[2,64,4096]{2,1,0:T(8,128)}) custom-call(f32[2,8,16,1024]{3,2,1,0:T(8,128)} %bitcast.3, f32[8,64,4096]{2,1,0:T(8,128)} %cells_hbm.1, ...), custom_call_target="tpu_custom_call" | custom-call | flops 1000000000 | bytes 100000000 | tf_op jit(solution)/shard_map/forward_lines/pallas_call | solution.py:448
  62.7 0.0 copy-start.2
  62.7 0.0 copy-start.3
  62.7 15.3 %fine_levels.1 = (f32[8,64,4096]{2,1,0:T(8,128)}, f32[2,16,1024]{2,1,0:T(8,128)}) custom-call(f32[8]{0:T(128)} %rate_ref.1, f32[8,64,4096]{2,1,0:T(8,128)} %cells_hbm.1, f32[8,64,128]{2,1,0:T(8,128)} %get-tuple-element.10.edge_ref, f32[8,1,4096]{2,1,0:T(1,128)} %get-tuple-element.11.south_ref, f32[8,1,4096]{2,1,0:T(1,128)} %get-tuple-element.12.north_ref, ...), custom_call_target="tpu_custom_call" | custom-call | flops 1000000000 | bytes 40000000 | tf_op jit(solution)/shard_map/fine_levels/pallas_call | solution.py:906
  79.3 0.0 copy-done.2
  79.3 0.0 copy-done.3
  79.4 0.0 copy-start
  79.4 1.2 %copy-done = f32[1,2,8,16,1024]{4,3,2,1,0:T(8,128)S(1)} copy-done((f32[1,2,8,16,1024]{4,3,2,1,0:T(8,128)S(1)}, f32[1,2,8,16,1024]{4,3,2,1,0:T(8,128)}, u32[]{:S(2)}) %copy-start) | copy-done | bytes 1048600
  80.6 0.0 copy-start.1
  80.6 0.9 copy-done.1
  81.5 21.2 %backward_lines.1 = f32[2,8,16,1024]{3,2,1,0:T(8,128)S(1)} custom-call(f32[1]{0:T(128)S(6)} %copy.17.refs_0_, f32[2,16,1024]{2,1,0:T(8,128)S(1)} %copy-done.1, f32[2,8,16,1024]{3,2,1,0:T(8,128)S(1)} %bitcast.4, f32[1,1024]{1,0:T(1,128)S(1)} %multiply_exponential_fusion.refs_3_, f32[2,32,128]{2,1,0:T(8,128)S(1)} %copy-done.3, bf16[256,768]{1,0:T(8,128)(2,1)S(1)} %copy-done.2), custom_call_target="tpu_custom_call" | custom-call | flops 1000000000 | bytes 50000000 | tf_op jit(solution)/shard_map/backward_lines/pallas_call | solution.py:655
  102.7 1.0 copy.18
  (1 shorter events, 0.0 us)
Async XLA Ops:
  62.7 16.7 %copy-start.2 = (bf16[256,768]{1,0:T(8,128)(2,1)S(1)}, bf16[256,768]{1,0:T(8,128)(2,1)}, u32[]{:S(2)}) copy-start(bf16[256,768]{1,0:T(8,128)(2,1)} %constant.40.clone.refs_5_) | copy-start | bytes 1179652
  62.7 16.7 %copy-start.3 = (f32[2,32,128]{2,1,0:T(8,128)S(1)}, f32[2,32,128]{2,1,0:T(8,128)}, u32[]{:S(2)}) copy-start(f32[2,32,128]{2,1,0:T(8,128)} %constant.39.clone.refs_4_) | copy-start | bytes 98308
  79.4 1.2 %copy-start = (f32[1,2,8,16,1024]{4,3,2,1,0:T(8,128)S(1)}, f32[1,2,8,16,1024]{4,3,2,1,0:T(8,128)}, u32[]{:S(2)}) copy-start(f32[1,2,8,16,1024]{4,3,2,1,0:T(8,128)} %param.13) | copy-start | bytes 3145732
  80.6 0.9 copy-start.1

commit v3 on v2

--- a/solution.py
+++ b/solution.py
@@ -9,6 +9,7 @@
 from jax.sharding import PartitionSpec as P
 
 RATIO = 4
+LATE_PIECES = 6
 
 
 fine_step = 0.1
@@ -163,7 +164,9 @@
     edge_ref,
     south_ref,
     north_ref,
-    outer_ref,
+    under_ref,
+    over_ref,
+    low_ref,
     pencil,
     mid,
     turn,
@@ -193,6 +196,8 @@
     col_recv,
     outer_send,
     outer_recv,
+    late,
+    late_sem,
 ):
     mine, at, half = lax.axis_index("grp"), lax.axis_index("gx"), lax.axis_index("gy")
     above, below = lax.rem(half + 1, halves_y), lax.rem(half + halves_y - 1, halves_y)
@@ -217,7 +222,11 @@
             )
         )
     ]
-    for load in loads:
+    early_rows = over_ref.shape[1]
+    late_rows = pl.ds(early_rows, fine_rows - early_rows)
+    late_in = pltpu.make_async_copy(cells_ref.at[0, late_rows, :], late, late_sem.at[0])
+    late_out = pltpu.make_async_copy(late, low_ref.at[0], late_sem.at[1])
+    for load in loads + [late_in]:
         load.start()
     greet(groups, columns, (above, below))
 
@@ -243,36 +252,33 @@
             device_id_type=MESH,
         )
 
-    def outer_copies(piece):
-        row = pl.ds(piece * SUBLANES, SUBLANES)
-        return [
-            pltpu.make_async_remote_copy(
-                src_ref=cells_ref.at[(levels - 1, 0)[k], row, :],
-                dst_ref=outer_ref.at[k, row, :],
-                send_sem=outer_send.at[k, piece],
-                recv_sem=outer_recv.at[k, piece],
-                device_id={"grp": lax.rem(mine + (1, groups - 1)[k], groups)},
-                device_id_type=MESH,
-            )
-            for k in range(2)
-        ]
-
-    pieces = fine_rows // SUBLANES
-    ahead = min(4, pieces)
-    during = min(turns, pieces - ahead)
-
-    def start_outer(piece):
-        for copy in outer_copies(piece):
-            copy.start()
+    def outer_copy(k, piece):
+        row = pl.ds(pl.multiple_of(piece * SUBLANES, SUBLANES), SUBLANES)
+        return pltpu.make_async_remote_copy(
+            src_ref=cells_ref.at[(levels - 1, 0)[k], row, :],
+            dst_ref=(under_ref, over_ref)[k].at[0, row, :],
+            send_sem=outer_send.at[k, piece],
+            recv_sem=outer_recv.at[k, piece],
+            device_id={"grp": lax.rem(mine + (1, groups - 1)[k], groups)},
+            device_id_type=MESH,
+        )
+
+    pieces = (fine_rows // SUBLANES, early_rows // SUBLANES)
+    during = min(turns, pieces[0])
+    ahead = pieces[0] - during
 
     for i in range(turns):
         for d in range(columns):
             first_copy(i, (d + 1) % columns).start()
-    for piece in range(ahead):
-        start_outer(piece)
-
-    for load in loads:
+    for piece in range(max(ahead, pieces[1])):
+        if piece < ahead:
+            outer_copy(0, piece).start()
+        if piece < pieces[1]:
+            outer_copy(1, piece).start()
+
+    for load in loads + [late_in]:
         load.wait()
+    late_out.start()
     lane_at = lax.broadcasted_iota(jnp.int32, (fine_rows, LANES), 1)
     for level in range(levels):
         row_out[0, level : level + 1, :] = edge_rows[0, level, SUBLANES - 1 : SUBLANES, :]
@@ -344,14 +350,22 @@
             pl.when(stays)(lambda: local().start())
             pl.when(jnp.logical_not(stays))(lambda: remote().start())
         if during == turns:
-            start_outer(ahead + i)
+            outer_copy(0, ahead + i).start()
         else:
-            pl.when(i < during)(lambda: start_outer(ahead + i))
+            pl.when(i < during)(lambda: outer_copy(0, ahead + i).start())
         return carry
 
     lax.fori_loop(0, turns, one_turn, 0)
-    for piece in range(ahead + during, pieces):
-        start_outer(piece)
+    for copy in outer:
+        copy.wait()
+    for level in range(levels):
+        south_ref[level] = row_in[0, level : level + 1, :]
+        north_ref[level] = row_in[1, level : level + 1, :]
+        edge_ref[level] = jnp.where(
+            lane_at < LANES // 2,
+            col_in[1, :, level : level + 1],
+            col_in[0, :, level : level + 1],
+        )
     for field in range(groups):
         for inner in range(blocks):
             plane, row = inner // row_blocks, inner % row_blocks * SUBLANES
@@ -379,16 +393,6 @@
     for field in range(groups - 1):
         for plane in range(quarter):
             rim_ref[field, plane, 0:rows, :] = scale * landed[field, plane]
-    for copy in outer:
-        copy.wait()
-    for level in range(levels):
-        south_ref[level] = row_in[0, level : level + 1, :]
-        north_ref[level] = row_in[1, level : level + 1, :]
-        edge_ref[level] = jnp.where(
-            lane_at < LANES // 2,
-            col_in[1, :, level : level + 1],
-            col_in[0, :, level : level + 1],
-        )
     for side in sides:
         side.wait()
     rest = rim_ref.shape[2] - rows - 2
@@ -414,9 +418,10 @@
         heat = near * heat + far * (before + after)
         heat = near * pltpu.roll(heat, span - 1, 1) + far * (heat + pltpu.roll(heat, span - 2, 1))
         heat_ref[plane] = heat[:, :width]
-    for piece in range(pieces):
-        for copy in outer_copies(piece):
-            copy.wait()
+    late_out.wait()
+    for k in range(2):
+        for piece in range(pieces[k]):
+            outer_copy(k, piece).wait()
     for i in range(turns):
         for d in range(1, columns):
             first_copy(i, d).wait_send()
@@ -431,7 +436,7 @@
     return near, (1.0 - near) / 2.0
 
 
-def forward(modes, cells, groups, columns, halves_y):
+def forward(modes, cells, early_rows, groups, columns, halves_y):
     _, planes, rows, width = modes.shape
     levels, fine_rows, fine_cols = cells.shape
     length = width * columns
@@ -454,10 +459,12 @@
             jax.ShapeDtypeStruct((levels, fine_rows, LANES), jnp.float32),
             jax.ShapeDtypeStruct((levels, 1, fine_cols), jnp.float32),
             jax.ShapeDtypeStruct((levels, 1, fine_cols), jnp.float32),
-            jax.ShapeDtypeStruct((2, fine_rows, fine_cols), jnp.float32),
+            jax.ShapeDtypeStruct((1, fine_rows, fine_cols), jnp.float32),
+            jax.ShapeDtypeStruct((1, early_rows, fine_cols), jnp.float32),
+            jax.ShapeDtypeStruct((1, fine_rows - early_rows, fine_cols), jnp.float32),
         ],
         in_specs=[pl.BlockSpec(memory_space=pltpu.HBM)] * 4,
-        out_specs=[vmem] * 5 + [pl.BlockSpec(memory_space=pltpu.HBM)],
+        out_specs=[vmem] * 5 + [pl.BlockSpec(memory_space=pltpu.HBM)] * 3,
         scratch_shapes=[
             pltpu.VMEM((turns, 2, SUBLANES, length), jnp.float32),
             pltpu.VMEM((2, SUBLANES * count, LANES), jnp.float32),
@@ -488,6 +495,8 @@
             dma((2,)),
             dma((2, fine_rows // SUBLANES)),
             dma((2, fine_rows // SUBLANES)),
+            pltpu.VMEM((fine_rows - early_rows, fine_cols), jnp.float32),
+            dma((2,)),
         ],
         compiler_params=pltpu.CompilerParams(
             collective_id=0, has_side_effects=True, vmem_limit_bytes=63 * 2**20
@@ -589,49 +598,72 @@
         else:
             pl.when(at + columns * slot < blocks)(work)
 
-    def arrival(group, block):
-        plane, row = where_is(block)
-        target = spectrum.at[:, group * quarter + plane, pl.ds(row, SUBLANES), :]
+    def where_at(group, k):
+        block = lax.rem(at + k, blocks)
+        plane = group * quarter + block // row_blocks
+        row = pl.multiple_of(lax.rem(block, row_blocks) * SUBLANES, SUBLANES)
+        return block, plane, pl.ds(row, SUBLANES)
+
+    def arrival(group, k):
+        block, plane, at_rows = where_at(group, k)
+        target = spectrum.at[:, plane, at_rows, :]
         return pltpu.make_async_copy(target, target, recv_two.at[group, block])
 
-    def onward(block, d):
-        plane, row = where_is(block)
-        target = spectrum.at[:, mine * quarter + plane, pl.ds(row, SUBLANES), :]
+    def onward(group, k, other, slot):
+        block, plane, at_rows = where_at(group, k)
+        target = spectrum.at[:, plane, at_rows, :]
         return pltpu.make_async_remote_copy(
             src_ref=target,
             dst_ref=target,
-            send_sem=send_three.at[block, d],
-            recv_sem=recv_two.at[mine, block],
-            device_id={"grp": lax.rem(mine + d, groups)},
+            send_sem=send_three.at[k, slot],
+            recv_sem=recv_two.at[group, block],
+            device_id={"grp": other},
             device_id_type=MESH,
         )
 
-    def finish(group, block):
-        plane, row = where_is(block)
-        index = group * quarter + plane
-        for k in range(2):
-            at_rows = pl.ds(row, SUBLANES)
-            out_ref[k, index, at_rows, :] = (
-                damp_ref[...] * modes_ref[k, index, at_rows, :]
-                + rates_ref[0] * spectrum[k, index, at_rows, :]
+    def finish(group, k):
+        _, index, at_rows = where_at(group, k)
+        for part in range(2):
+            out_ref[part, index, at_rows, :] = (
+                damp_ref[...] * modes_ref[part, index, at_rows, :]
+                + rates_ref[0] * spectrum[part, index, at_rows, :]
             )
 
-    for block in range(blocks):
-        arrival(mine, block).wait()
-        for d in range(1, groups):
-            onward(block, d).start()
-    for block in range(blocks):
-        finish(mine, block)
-    for block in range(blocks):
-        for d in range(1, groups):
-            group = lax.rem(mine + d, groups)
-            arrival(group, block).wait()
-            finish(group, block)
+    square = groups == 4
+    if square:
+        pair = mine + 1 - 2 * lax.rem(mine, 2)
+        across = lax.rem(mine + 2, groups)
+        others = [pair, across, lax.rem(pair + 2, groups)]
+        direct = 2
+    else:
+        others = [lax.rem(mine + d, groups) for d in range(1, groups)]
+        direct = groups - 1
+    sent = []
+    for k in range(blocks):
+        arrival(mine, k).wait()
+        for slot in range(direct):
+            copy = onward(mine, k, others[slot], slot)
+            copy.start()
+            sent.append(copy)
+    for k in range(blocks):
+        finish(mine, k)
+    for k in range(blocks):
+        for slot in range(direct):
+            arrival(others[slot], k).wait()
+            if square and slot == k % 2:
+                copy = onward(others[slot], k, others[1 - slot], 2)
+                copy.start()
+                sent.append(copy)
+    for slot in range(groups - 1):
+        for k in range(blocks):
+            if slot >= direct:
+                arrival(others[slot], k).wait()
+            finish(others[slot], k)
+    for copy in sent:
+        copy.wait_send()
     for block in range(blocks):
         remote, _, stays = to_worker(block)
         pl.when(jnp.logical_not(stays))(lambda: remote().wait_send())
-        for d in range(1, groups):
-            onward(block, d).wait_send()
     for slot in range(slots):
         for b in range(columns):
             remote, _, stays = to_owner(slot, b)
@@ -737,7 +769,8 @@
     edge_ref,
     south_ref,
     north_ref,
-    beyond_hbm,
+    under_hbm,
+    over_hbm,
     rim_ref,
     heat_ref,
     ty_ref,
@@ -746,6 +779,7 @@
     rx_ref,
     out_hbm,
     coarse_ref,
+    factor_ref,
     held,
     vel,
     acc,
@@ -761,31 +795,43 @@
     pieces = vel.shape[0]
     half = LANES // 2
 
-    def load(source, index, tile, slab):
-        return pltpu.make_async_copy(
-            source.at[index, :, pl.ds(pl.multiple_of(tile * LANES, LANES), LANES)],
-            held.at[slab, tile, pl.ds(SUBLANES, rows), :],
-            in_sem.at[slab],
-        )
-
-    def start_slab(source, index, slab):
-        @pl.loop(0, tiles)
+    early = over_hbm.shape[1]
+
+    near = min(RATIO + 1, levels)
+    groups = (
+        (under_hbm, 0, 1, 0),
+        (cells_hbm, 0, near, 1),
+        (cells_hbm, near, levels - near, near + 1),
+        (over_hbm, 0, 1, slabs - 1),
+    )
+
+    def start_group(k):
+        source, first, depth, slab = groups[k]
+
+        @pl.loop(0, tiles if depth else 0)
         def _(tile):
-            load(source, index, tile, slab).start()
-
-    def wait_slab(slab):
-        whole = held.at[slab, pl.ds(0, tiles), pl.ds(SUBLANES, rows), :]
-        pltpu.make_async_copy(whole, whole, in_sem.at[slab]).wait()
+            pltpu.make_async_copy(
+                source.at[
+                    pl.ds(first, depth), :, pl.ds(pl.multiple_of(tile * LANES, LANES), LANES)
+                ],
+                held.at[pl.ds(slab, depth), tile, pl.ds(SUBLANES, source.shape[1]), :],
+                in_sem.at[k],
+            ).start()
+
+    def wait_group(k):
+        source, _, depth, slab = groups[k]
+        if depth:
+            whole = held.at[
+                pl.ds(slab, depth), pl.ds(0, tiles), pl.ds(SUBLANES, source.shape[1]), :
+            ]
+            pltpu.make_async_copy(whole, whole, in_sem.at[k]).wait()
 
     @pl.when(plane == 0)
     def _():
-        start_slab(beyond_hbm, 0, 0)
-
-        @pl.loop(0, levels)
-        def _(level):
-            start_slab(cells_hbm, level, level + 1)
-
-        start_slab(beyond_hbm, 1, slabs - 1)
+        start_group(0)
+        start_group(1)
+        empty = jnp.zeros((tiles, rows - early, LANES), jnp.float32)
+        held[slabs - 1, 0:tiles, SUBLANES + early : SUBLANES + rows, :] = empty
 
     for part in range(RATIO):
         level = plane * RATIO + part
@@ -814,11 +860,17 @@
 
     @pl.when(plane == 0)
     def _():
-        wait_slab(0)
-        wait_slab(1)
-
-    for part in range(RATIO):
-        wait_slab(plane * RATIO + part + 2)
+        start_group(2)
+        start_group(3)
+        wait_group(0)
+        wait_group(1)
+
+    top_plane = plane == pl.num_programs(0) - 1
+
+    @pl.when(plane == (1 if levels > RATIO else 0))
+    def _():
+        wait_group(2)
+        wait_group(3)
 
     side_rates = [fine_step * rate_ref[plane * RATIO + part] for part in range(RATIO)]
     own_rates = [1.0 - 6.0 * rate for rate in side_rates]
@@ -881,18 +933,27 @@
         lanes = slice(k * LANES, (k + 1) * LANES)
         coarse_ref[0, :, lanes] = heat_ref[0, :, lanes] - cells
 
-    @pl.when(plane == pl.num_programs(0) - 1)
+    @pl.when(top_plane)
+    def _():
+        wide = vel.shape[2]
+        for k in range(pieces):
+            factor_ref[:, k * wide : (k + 1) * wide] = (
+                side_rates[RATIO - 1] - vel[k, (fields - 1) * rows + early : fields * rows, :]
+            )
+
+    @pl.when(top_plane)
     def _():
         for index in range(levels // RATIO):
             for s in range(strips):
                 out_copy(index, s).wait()
 
 
-def fine_update(rimmed, heat, edge, south, north, beyond, salinity, diffusivity):
+def fine_update(rimmed, heat, edge, south, north, under, over, salinity, diffusivity):
     levels, rows, cols = salinity.shape
     fields, quarter = rimmed.shape[:2]
     row_count, width = rows // RATIO, cols // RATIO
     cell_count = LANES // 2
+    late_rows = rows - over.shape[1]
     ty = rows_table(row_count, rimmed.shape[2])
     tx = lanes_table(cell_count)
     ry = average_table(rows, 1.0 / RATIO).T
@@ -914,6 +975,7 @@
             pl.BlockSpec((RATIO, 1, cols), lambda i: (i, 0, 0)),
             pl.BlockSpec((RATIO, 1, cols), lambda i: (i, 0, 0)),
             hbm,
+            hbm,
             pl.BlockSpec((fields, 1) + rimmed.shape[2:], lambda i: (0, i, 0, 0)),
             pl.BlockSpec((1, row_count, width), lambda i: (i, 0, 0)),
             fixed(ty),
@@ -921,35 +983,126 @@
             fixed(ry),
             fixed(rx),
         ],
-        out_specs=[hbm, pl.BlockSpec((1, row_count, width), lambda i: (i, 0, 0))],
+        out_specs=[
+            hbm,
+            pl.BlockSpec((1, row_count, width), lambda i: (i, 0, 0)),
+            pl.BlockSpec((late_rows, cols), lambda i: (0, 0)),
+        ],
         out_shape=[
             jax.ShapeDtypeStruct(salinity.shape, jnp.float32),
             jax.ShapeDtypeStruct((quarter, row_count, width), jnp.float32),
+            jax.ShapeDtypeStruct((late_rows, cols), jnp.float32),
         ],
         scratch_shapes=[
             pltpu.VMEM((levels + 2, cols // LANES + 1, rows + 2 * SUBLANES, LANES), jnp.float32),
             pltpu.VMEM((pieces, fields * rows, cell_count * RATIO), jnp.float32),
             pltpu.VMEM((rows, cols), jnp.float32),
             pltpu.VMEM((levels, rows, cols), jnp.float32),
-            pltpu.SemaphoreType.DMA((levels + 2,)),
+            pltpu.SemaphoreType.DMA((4,)),
             pltpu.SemaphoreType.DMA((quarter, rows // SUBLANES)),
         ],
         compiler_params=pltpu.CompilerParams(
-            dimension_semantics=("arbitrary",), vmem_limit_bytes=63 * 2**20
+            dimension_semantics=("arbitrary",), vmem_limit_bytes=59 * 2**20
         ),
         cost_estimate=pl.CostEstimate(flops=10**9, bytes_accessed=4 * 10**7, transcendentals=0),
-    )(diffusivity, salinity, edge, south, north, beyond, rimmed, heat, ty, tx, ry, rx)
+    )(diffusivity, salinity, edge, south, north, under, over, rimmed, heat, ty, tx, ry, rx)
+
+
+def outer_kernel(
+    level_hbm,
+    factor_hbm,
+    over_hbm,
+    cells_hbm,
+    ry_hbm,
+    rx_hbm,
+    out_hbm,
+    coarse_ref,
+    held,
+    factor_ref,
+    over_ref,
+    ry_ref,
+    rx_ref,
+    in_sem,
+    out_sem,
+):
+    levels, rows = out_hbm.shape[:2]
+    late = held.shape[0]
+    plane = coarse_ref.shape[0] - 1
+    place = out_hbm.at[levels - 1, pl.ds(rows - late, late), :]
+    pairs = (
+        (factor_hbm, factor_ref),
+        (over_hbm.at[0], over_ref),
+        (ry_hbm, ry_ref),
+        (rx_hbm, rx_ref),
+        (place, held),
+        (cells_hbm, coarse_ref),
+    )
+    loads = [
+        pltpu.make_async_copy(source, target, in_sem.at[k])
+        for k, (source, target) in enumerate(pairs)
+    ]
+    for load in loads:
+        load.start()
+    for load in loads:
+        load.wait()
+    added = factor_ref[...] * over_ref[...]
+    held[...] = held[...] + added
+    store = pltpu.make_async_copy(held, place, out_sem.at[0])
+    store.start()
+    for k, cells in enumerate(block_means(added, ry_ref, rx_ref)):
+        lanes = slice(k * LANES, (k + 1) * LANES)
+        coarse_ref[plane, :, lanes] = coarse_ref[plane, :, lanes] - cells
+    store.wait()
+
+
+def outer_update(levels_next, factor, over, cells):
+    rows = levels_next.shape[1]
+    late = factor.shape[0]
+    ry = average_table(rows, 1.0 / RATIO)[rows - late : rows].T
+    ry = np.concatenate([ry, ry], axis=1)
+    rx = average_table(LANES * RATIO, 1.0 / RATIO / RATIO)
+    hbm = pl.BlockSpec(memory_space=pltpu.HBM)
+    return pl.pallas_call(
+        outer_kernel,
+        name="outer_levels",
+        in_specs=[hbm] * 6,
+        out_specs=[hbm, pl.BlockSpec(memory_space=pltpu.VMEM)],
+        out_shape=[
+            jax.ShapeDtypeStruct(levels_next.shape, jnp.float32),
+            jax.ShapeDtypeStruct(cells.shape, jnp.float32),
+        ],
+        scratch_shapes=[
+            pltpu.VMEM(factor.shape, jnp.float32),
+            pltpu.VMEM(factor.shape, jnp.float32),
+            pltpu.VMEM(factor.shape, jnp.float32),
+            pltpu.VMEM(ry.shape, jnp.bfloat16),
+            pltpu.VMEM(rx.shape, jnp.bfloat16),
+            pltpu.SemaphoreType.DMA((6,)),
+            pltpu.SemaphoreType.DMA((1,)),
+        ],
+        input_output_aliases={0: 0},
+        compiler_params=pltpu.CompilerParams(vmem_limit_bytes=59 * 2**20),
+        cost_estimate=pl.CostEstimate(flops=10**8, bytes_accessed=4 * 10**6, transcendentals=0),
+    )(levels_next, factor, over, cells, ry, rx)
+
+
+def from_above(layer, axis):
+    count = lax.axis_size(axis)
+    return lax.ppermute(layer, axis, [((i + 1) % count, i) for i in range(count)])
 
 
 def per_device(coarse_modes, salinity, viscosity, forcing_gain, diffusivity):
     width = coarse_modes.shape[4]
     groups, columns = lax.axis_size("grp"), lax.axis_size("gx")
-    rimmed, heat, edge, south, north, beyond = forward(
-        coarse_modes[0], salinity, groups, columns, lax.axis_size("gy")
+    early_rows = salinity.shape[1] - LATE_PIECES * SUBLANES
+    rimmed, heat, edge, south, north, under, over, low = forward(
+        coarse_modes[0], salinity, early_rows, groups, columns, lax.axis_size("gy")
     )
-    salinity_next, restricted = fine_update(
-        rimmed, heat, edge, south, north, beyond, salinity, diffusivity
+    over_late = from_above(low, "grp")
+    partial_next, partial_cells, factor = fine_update(
+        rimmed, heat, edge, south, north, under, over, salinity, diffusivity
     )
+    salinity_next, restricted = outer_update(partial_next, factor, over_late, partial_cells)
     total_modes = width * columns
     mode_index = lax.axis_index("gx") * width + lax.broadcasted_iota(jnp.int32, (1, width), 1)
     wavenumber = jnp.where(mode_index < total_modes // 2, mode_index, mode_index - total_modes)

time: 104 us -> 97.8 us (0.940)
  Pallas kernels: 98.5 us -> 87.7 us
  starting transfers between devices: 0 us -> 3.2 us
  waiting for transfers between devices: 0 us -> 1.48 us
    pallas_call x1, Pallas kernels: 62 us -> 46.8 us  [forward(): pl.pallas_call(lambda *refs: forward_kernel(groups, columns, halves_y, *r...]
    pallas_call x0 -> x1, Pallas kernels: none -> 3.43 us  [outer_update(): pl.pallas_call(outer_kernel, name='outer_levels', in_specs=[hbm] * 6, out...]
    ppermute x0 -> x1, starting transfers between devices: none -> 3.2 us  [from_above(): lax.ppermute(layer, axis, [((i + 1) % count, i) for i in range(count)])]
    pallas_call x1, Pallas kernels: 21.2 us -> 22.8 us  [backward(): pl.pallas_call(lambda *refs: backward_kernel(groups, columns, *refs), nam...]
    ppermute x0 -> x1, waiting for transfers between devices: none -> 1.48 us  [from_above(): lax.ppermute(layer, axis, [((i + 1) % count, i) for i in range(count)])]
    unnamed x9 -> x11, local copies, waits for them, and re-layouts: 3.11 us -> 2.78 us
  transfers between devices with their start and end apart: 0 -> 1, of which waited for: 0 -> 1; matrix products, arithmetic and copies ran while one was open for 0% -> 0% of each run, Pallas kernels for 0% -> 15%
where the time goes in v3:
time: 97.8 us; the launch traced here: 97.2 us
  Pallas kernels  87.7 us (90%)
  starting transfers between devices  3.2 us (3%)
  local copies, waits for them, and re-layouts  2.78 us (3%)
  between operations  2.03 us (2%)
  waiting for transfers between devices  1.48 us (2%)
    pallas_call x1, Pallas kernels, forward(): pl.pallas_call(lambda *refs: forward_kernel(groups, columns, halves_y, *r...  46.8 us
    pallas_call x1, Pallas kernels, backward(): pl.pallas_call(lambda *refs: backward_kernel(groups, columns, *refs), nam...  22.8 us
    pallas_call x1, Pallas kernels, fine_update(): pl.pallas_call(fine_kernel, name='fine_levels', grid=(quarter,), in_specs...  14.8 us
    pallas_call x1, Pallas kernels, outer_update(): pl.pallas_call(outer_kernel, name='outer_levels', in_specs=[hbm] * 6, out...  3.43 us
    ppermute x1, starting transfers between devices, from_above(): lax.ppermute(layer, axis, [((i + 1) % count, i) for i in range(count)])  3.2 us
    unnamed x11, local copies, waits for them, and re-layouts  2.78 us
  transfers between devices with their start and end apart: 1, of which 1 were waited for; matrix products, arithmetic and copies ran while one was open for 0% of the time, Pallas kernels for 15%

profile of v3, /device:TPU:0, one launch (start us, length us, event | category | flops | bytes accessed | tf_op | source)
XLA Modules:
  0.0 97.2 jit_solution(17413963912979953225)
XLA Ops:
  0.6 46.8 %forward_lines.1 = (f32[3,2,32,1152]{3,2,1,0:T(8,128)}, f32[2,16,1024]{2,1,0:T(8,128)}, f32[8,64,128]{2,1,0:T(8,128)}, f32[8,1,4096]{2,1,0:T(1,128)}, f32[8,1,40...) custom-call(f32[2,8,16,1024]{3,2,1,0:T(8,128)} %bitcast.3, ...), custom_call_target="tpu_custom_call" | custom-call | flops 1000000000 | bytes 100000000 | tf_op jit(solution)/shard_map/forward_lines/pallas_call | solution.py:453
  47.4 3.2 %collective-permute-start = (f32[1,48,4096]{2,1,0:T(8,128)}, f32[1,48,4096]{2,1,0:T(8,128)S(1)}, u32[]{:S(2)}, u32[]{:S(2)}) collective-permute-start(f32[1,48,4096]{2,1,0:T(8,128)} %get-tuple-element.24), channel_id=1, source_target_pairs={{8,0},{16,8},{24,16},{0,24},{9,1},{17,9},{25,17},{1,25},{10,2},{18... | collective-permute-start | bytes 2359304 | tf_op jit(solution)/shard_map/ppermute | solution.py:1091
  51.9 0.0 copy-start
  51.9 0.0 copy-start.2
  51.9 0.0 copy-start.3
  51.9 14.8 %fine_levels.1 = (f32[8,64,4096]{2,1,0:T(8,128)}, f32[2,16,1024]{2,1,0:T(8,128)}, f32[48,4096]{1,0:T(8,128)}) custom-call(f32[8]{0:T(128)} %rate_ref.1, f32[8,64,4096]{2,1,0:T(8,128)} %cells_hbm.1, f32[8,64,128]{2,1,0:T(8,128)} %get-tuple-element.15.edge_ref, f32[8,1,4096]{2,1,0:T(1,128)} %get-tuple-element.16.south_ref, ...), custom_call_target="tpu_custom_call" | custom-call | flops 1000000000 | bytes 40000000 | tf_op jit(solution)/shard_map/fine_levels/pallas_call | solution.py:967
  66.8 1.5 %collective-permute-done.over_hbm = f32[1,48,4096]{2,1,0:T(8,128)S(1)} collective-permute-done((f32[1,48,4096]{2,1,0:T(8,128)}, f32[1,48,4096]{2,1,0:T(8,128)S(1)}, u32[]{:S(2)}, u32[]{:S(2)}) %collective-permute-start) | collective-permute-done | bytes 786464 | tf_op jit(solution)/shard_map/ppermute | solution.py:1091
  68.2 0.0 copy-start.4
  68.2 0.9 copy-done.4
  69.1 3.4 %outer_levels.1 = (f32[8,64,4096]{2,1,0:T(8,128)}, f32[2,16,1024]{2,1,0:T(8,128)}) custom-call(f32[8,64,4096]{2,1,0:T(8,128)} %get-tuple-element.22.level_hbm, f32[48,4096]{1,0:T(8,128)} %get-tuple-element.23.factor_hbm, f32[1,48,4096]{2,1,0:T(8,128)} %copy-done.4, f32[2,16,1024]{2,1,0:T(8,128)} %get-tuple-element.25.cells_hbm, ...), custom_call_target="tpu_custom_call", output_to_operand_aliasing={{0}: (0, {})} | custom-call | flops 100000000 | bytes 4000000 | tf_op jit(solution)/shard_map/outer_levels/pallas_call | solution.py:1065
  72.6 0.0 copy-done
  72.6 0.0 copy-done.2
  72.6 0.0 copy-done.3
  72.6 0.0 copy-start.1
  72.6 0.9 copy-done.1
  73.5 22.8 %backward_lines.1 = f32[2,8,16,1024]{3,2,1,0:T(8,128)S(1)} custom-call(f32[1]{0:T(128)S(6)} %copy.21.refs_0_, f32[2,16,1024]{2,1,0:T(8,128)S(1)} %copy-done.1, f32[2,8,16,1024]{3,2,1,0:T(8,128)S(1)} %bitcast.4, f32[1,1024]{1,0:T(1,128)S(1)} %multiply_exponential_fusion.refs_3_, f32[2,32,128]{2,1,0:T(8,128)S(1)} %copy-done.3, bf16[256,768]{1,0:T(8,128)(2,1)S(1)} %copy-done.2), custom_call_target="tpu_custom_call" | custom-call | flops 1000000000 | bytes 50000000 | tf_op jit(solution)/shard_map/backward_lines/pallas_call | solution.py:687
  96.3 1.0 %copy.22 = f32[1,2,8,16,1024]{4,3,2,1,0:T(8,128)} copy(f32[1,2,8,16,1024]{4,3,2,1,0:T(8,128)S(1)} %bitcast.5) | data formatting | bytes 2097152
  (1 shorter events, 0.0 us)
Async XLA Ops:
  47.4 20.8 %collective-permute-start = (f32[1,48,4096]{2,1,0:T(8,128)}, f32[1,48,4096]{2,1,0:T(8,128)S(1)}, u32[]{:S(2)}, u32[]{:S(2)}) collective-permute-start(f32[1,48,4096]{2,1,0:T(8,128)} %get-tuple-element.24), channel_id=1, source_target_pairs={{8,0},{16,8},{24,16},{0,24},{9,1},{17,9},{25,17},{1,25},{10,2},{18... | collective-permute-start | bytes 2359304 | tf_op jit(solution)/shard_map/ppermute | solution.py:1091
  51.9 20.7 %copy-start = (f32[1,2,8,16,1024]{4,3,2,1,0:T(8,128)S(1)}, f32[1,2,8,16,1024]{4,3,2,1,0:T(8,128)}, u32[]{:S(2)}) copy-start(f32[1,2,8,16,1024]{4,3,2,1,0:T(8,128)} %param.15) | copy-start | bytes 3145732
  51.9 20.7 %copy-start.2 = (bf16[256,768]{1,0:T(8,128)(2,1)S(1)}, bf16[256,768]{1,0:T(8,128)(2,1)}, u32[]{:S(2)}) copy-start(bf16[256,768]{1,0:T(8,128)(2,1)} %constant.43.clone.refs_5_) | copy-start | bytes 1179652
  51.9 20.7 %copy-start.3 = (f32[2,32,128]{2,1,0:T(8,128)S(1)}, f32[2,32,128]{2,1,0:T(8,128)}, u32[]{:S(2)}) copy-start(f32[2,32,128]{2,1,0:T(8,128)} %constant.42.clone.refs_4_) | copy-start | bytes 98308
  68.2 0.9 copy-start.4
  72.6 0.9 copy-start.1

commit v4 on v3

--- a/solution.py
+++ b/solution.py
@@ -9,7 +9,7 @@
 from jax.sharding import PartitionSpec as P
 
 RATIO = 4
-LATE_PIECES = 6
+LATE_PIECES = 5
 
 
 fine_step = 0.1
@@ -1081,7 +1081,7 @@
             pltpu.SemaphoreType.DMA((1,)),
         ],
         input_output_aliases={0: 0},
-        compiler_params=pltpu.CompilerParams(vmem_limit_bytes=59 * 2**20),
+        compiler_params=pltpu.CompilerParams(vmem_limit_bytes=24 * 2**20),
         cost_estimate=pl.CostEstimate(flops=10**8, bytes_accessed=4 * 10**6, transcendentals=0),
     )(levels_next, factor, over, cells, ry, rx)
 

time: 97.8 us -> 97.1 us (level)
  Pallas kernels: 87.7 us -> 90.6 us
  starting transfers between devices: 3.2 us -> 1.13 us
  waiting for transfers between devices: 1.48 us -> 0.01 us
    pallas_call x1, Pallas kernels: 46.8 us -> 49 us  [forward(): pl.pallas_call(lambda *refs: forward_kernel(groups, columns, halves_y, *r...]
    ppermute x1, starting transfers between devices: 3.2 us -> 1.13 us  [from_above(): lax.ppermute(layer, axis, [((i + 1) % count, i) for i in range(count)])]
    pallas_call x1, Pallas kernels: 22.8 us -> 24.4 us  [backward(): pl.pallas_call(lambda *refs: backward_kernel(groups, columns, *refs), nam...]
    ppermute x1, waiting for transfers between devices: 1.48 us -> 0.01 us  [from_above(): lax.ppermute(layer, axis, [((i + 1) % count, i) for i in range(count)])]
    unnamed x11 -> x15, local copies, waits for them, and re-layouts: 2.78 us -> 2.99 us
  transfers between devices with their start and end apart: 1 -> 1, of which waited for: 1 -> 0; matrix products, arithmetic and copies ran while one was open for 0% -> 0% of each run, Pallas kernels for 15% -> 15%
where the time goes in v4:
time: 97.1 us; the launch traced here: 96.8 us
  Pallas kernels  90.6 us (93%)
  local copies, waits for them, and re-layouts  2.99 us (3%)
  between operations  2.07 us (2%)
  starting transfers between devices  1.13 us (1%)
    pallas_call x1, Pallas kernels, forward(): pl.pallas_call(lambda *refs: forward_kernel(groups, columns, halves_y, *r...  49 us
    pallas_call x1, Pallas kernels, backward(): pl.pallas_call(lambda *refs: backward_kernel(groups, columns, *refs), nam...  24.4 us
    pallas_call x1, Pallas kernels, fine_update(): pl.pallas_call(fine_kernel, name='fine_levels', grid=(quarter,), in_specs...  14.7 us
    unnamed x15, local copies, waits for them, and re-layouts  2.99 us
    pallas_call x1, Pallas kernels, outer_update(): pl.pallas_call(outer_kernel, name='outer_levels', in_specs=[hbm] * 6, out...  2.55 us
  transfers between devices with their start and end apart: 1, of which 0 were waited for; matrix products, arithmetic and copies ran while one was open for 0% of the time, Pallas kernels for 15%

profile of v4, /device:TPU:0, one launch (start us, length us, event | category | flops | bytes accessed | tf_op | source)
XLA Modules:
  0.0 96.8 jit_solution(3773534770415445615)
XLA Ops:
  0.6 0.0 copy-start.1
  0.6 0.0 copy-start.4
  0.7 49.0 %forward_lines.1 = (f32[3,2,32,1152]{3,2,1,0:T(8,128)}, f32[2,16,1024]{2,1,0:T(8,128)}, f32[8,64,128]{2,1,0:T(8,128)}, f32[8,1,4096]{2,1,0:T(1,128)}, f32[8,1,40...) custom-call(f32[2,8,16,1024]{3,2,1,0:T(8,128)} %bitcast.3, ...), custom_call_target="tpu_custom_call" | custom-call | flops 1000000000 | bytes 100000000 | tf_op jit(solution)/shard_map/forward_lines/pallas_call | solution.py:453
  49.6 1.1 %collective-permute-start = (f32[1,40,4096]{2,1,0:T(8,128)}, f32[1,40,4096]{2,1,0:T(8,128)S(1)}, u32[]{:S(2)}, u32[]{:S(2)}) collective-permute-start(f32[1,40,4096]{2,1,0:T(8,128)} %get-tuple-element.24), channel_id=1, source_target_pairs={{8,0},{16,8},{24,16},{0,24},{9,1},{17,9},{25,17},{1,25},{10,2},{18... | collective-permute-start | bytes 1966088 | tf_op jit(solution)/shard_map/ppermute | solution.py:1091
  52.1 0.0 copy-start
  52.1 0.0 copy-start.5
  52.1 0.0 copy-start.6
  52.1 14.7 %fine_levels.1 = (f32[8,64,4096]{2,1,0:T(8,128)}, f32[2,16,1024]{2,1,0:T(8,128)}, f32[40,4096]{1,0:T(8,128)}) custom-call(f32[8]{0:T(128)} %rate_ref.1, f32[8,64,4096]{2,1,0:T(8,128)} %cells_hbm.1, f32[8,64,128]{2,1,0:T(8,128)} %get-tuple-element.15.edge_ref, f32[8,1,4096]{2,1,0:T(1,128)} %get-tuple-element.16.south_ref, ...), custom_call_target="tpu_custom_call" | custom-call | flops 1000000000 | bytes 40000000 | tf_op jit(solution)/shard_map/fine_levels/pallas_call | solution.py:967
  66.9 0.0 collective-permute-done.over_hbm
  66.9 0.0 copy-done.1
  66.9 0.0 copy-done.4
  66.9 0.0 copy-start.2
  66.9 1.1 %copy-done.2 = f32[40,4096]{1,0:T(8,128)S(1)} copy-done((f32[40,4096]{1,0:T(8,128)S(1)}, f32[40,4096]{1,0:T(8,128)}, u32[]{:S(2)}) %copy-start.2) | copy-done | bytes 655384
  68.0 0.0 copy-start.3
  68.0 0.9 copy-done.3
  68.9 2.5 %outer_levels.1 = (f32[8,64,4096]{2,1,0:T(8,128)}, f32[2,16,1024]{2,1,0:T(8,128)S(1)}) custom-call(f32[8,64,4096]{2,1,0:T(8,128)} %get-tuple-element.22.level_hbm, f32[40,4096]{1,0:T(8,128)S(1)} %copy-done.2, f32[1,40,4096]{2,1,0:T(8,128)S(1)} %collective-permute-done.over_hbm, f32[2,16,1024]{2,1,0:T(8,128)S(1)} %copy-done.3, ...), custom_call_target="tpu_custom_call", output_to_operand_aliasing={{0}: (0, {})} | custom-call | flops 100000000 | bytes 4000000 | tf_op jit(solution)/shard_map/outer_levels/pallas_call | solution.py:1065
  71.5 0.0 copy-done
  71.5 0.0 copy-done.5
  71.5 0.0 copy-done.6
  71.5 24.4 %backward_lines.1 = f32[2,8,16,1024]{3,2,1,0:T(8,128)S(1)} custom-call(f32[1]{0:T(128)S(6)} %copy.21.refs_0_, f32[2,16,1024]{2,1,0:T(8,128)S(1)} %get-tuple-element.27.refs_1_, f32[2,8,16,1024]{3,2,1,0:T(8,128)S(1)} %bitcast.4, f32[1,1024]{1,0:T(1,128)S(1)} %multiply_exponential_fusion.refs_3_, f32[2,32,128]{2,1,0:T(8,128)S(1)} %copy-done.6, ...), custom_call_target="tpu_custom_call" | custom-call | flops 1000000000 | bytes 50000000 | tf_op jit(solution)/shard_map/backward_lines/pallas_call | solution.py:687
  95.8 1.0 %copy.22 = f32[1,2,8,16,1024]{4,3,2,1,0:T(8,128)} copy(f32[1,2,8,16,1024]{4,3,2,1,0:T(8,128)S(1)} %bitcast.5) | data formatting | bytes 2097152
  (1 shorter events, 0.0 us)
Async XLA Ops:
  0.6 66.3 %copy-start.1 = (bf16[1024,128]{1,0:T(8,128)(2,1)S(1)}, bf16[1024,128]{1,0:T(8,128)(2,1)}, u32[]{:S(2)}) copy-start(bf16[1024,128]{1,0:T(8,128)(2,1)} %constant.40.clone.rx_ref.rx_hbm) | copy-start | bytes 786436
  0.6 66.3 %copy-start.4 = (bf16[16,80]{1,0:T(8,128)(2,1)S(1)}, bf16[16,80]{1,0:T(8,128)(2,1)}, u32[]{:S(2)}) copy-start(bf16[16,80]{1,0:T(8,128)(2,1)} %constant.41.clone.ry_hbm) | copy-start | bytes 7684
  49.6 17.2 %collective-permute-start = (f32[1,40,4096]{2,1,0:T(8,128)}, f32[1,40,4096]{2,1,0:T(8,128)S(1)}, u32[]{:S(2)}, u32[]{:S(2)}) collective-permute-start(f32[1,40,4096]{2,1,0:T(8,128)} %get-tuple-element.24), channel_id=1, source_target_pairs={{8,0},{16,8},{24,16},{0,24},{9,1},{17,9},{25,17},{1,25},{10,2},{18... | collective-permute-start | bytes 1966088 | tf_op jit(solution)/shard_map/ppermute | solution.py:1091
  52.1 19.4 %copy-start = (f32[1,2,8,16,1024]{4,3,2,1,0:T(8,128)S(1)}, f32[1,2,8,16,1024]{4,3,2,1,0:T(8,128)}, u32[]{:S(2)}) copy-start(f32[1,2,8,16,1024]{4,3,2,1,0:T(8,128)} %param.15) | copy-start | bytes 3145732
  52.1 19.4 %copy-start.5 = (bf16[256,768]{1,0:T(8,128)(2,1)S(1)}, bf16[256,768]{1,0:T(8,128)(2,1)}, u32[]{:S(2)}) copy-start(bf16[256,768]{1,0:T(8,128)(2,1)} %constant.43.clone.refs_5_) | copy-start | bytes 1179652
  52.1 19.4 %copy-start.6 = (f32[2,32,128]{2,1,0:T(8,128)S(1)}, f32[2,32,128]{2,1,0:T(8,128)}, u32[]{:S(2)}) copy-start(f32[2,32,128]{2,1,0:T(8,128)} %constant.42.clone.refs_4_) | copy-start | bytes 98308
  66.9 1.1 %copy-start.2 = (f32[40,4096]{1,0:T(8,128)S(1)}, f32[40,4096]{1,0:T(8,128)}, u32[]{:S(2)}) copy-start(f32[40,4096]{1,0:T(8,128)} %get-tuple-element.23.factor_hbm) | copy-start | bytes 1966084
  68.0 0.9 copy-start.3
